TPU v7x, 128 devices: a whole 4x4x4 slice. The times are simulated.
128 devices in a mesh: row: 8 (over x, core), col: 16 (over z, y).
Axes of the slice: x: 4, y: 4, z: 4, core: 2. Of those that a mesh axis runs over, the one named last changes fastest.
Arguments:
- counts: float32 [8192, 8192], P('row', 'col'), may hold values from 0 to 514, as said below
- labels: int32 [983040], replicated, may hold values from 0 to 8191, as said below
- edge_tiles: int32 [4096, 2, 128], P(('row', 'col')), may hold values from 0 to 983039, as said below
- proposals: int32 [2, 256], replicated, may hold values from 0 to 8191, as said below
- accept_flags: int32 [256], P('col'), may hold values 0 or 1
Outputs:
- count_matrix: float32 [8192, 8192], P('row', 'col')
- merge_cost: float32 [256], P('col')
- accepted_cost: float32 [256], P('col')
Inputs may be any that keep to these rules, and one draw needn't show every extreme that they name: `counts`: Symmetric, whole numbers, every diagonal entry at least 2. `labels`: every block holds exactly 120 vertices. `edge_tiles`: each edge gives the two entries (label of its first vertex, label of its second) and the reverse; entry (r, s) lies in tile (r // 1024, s // 512). Of the 8192 entries of one device's edges at most 144 lie in one tile, and in every draw some tile gets exactly 144 entries from every device. proposals[1, p] differs from proposals[0, p]; for p // 16 = c, proposals[0, p] lies in c * 512 to (c + 1) * 512 - 1, and these sources are distinct.
All inputs are finite; a program needn't handle non-finite values. No bound on the sum of `accept_flags` on one device may be relied on, other than what follows from the above.
Results may differ from a plain program's by a relative error of at most 0.0003.
Values sent between devices are 32-bit elements; how exact they have to be, the bound alone decides.
A program may use at most 128 MiB of HBM per device.

v0:
```python
import jax
import jax.numpy as jnp
from jax import lax
from jax.sharding import PartitionSpec as P

BLOCKS = 8192
PROP_COL = 16


def in_blocks(shard, dim, devices):
    before, after = (shard.shape[:dim], shard.shape[dim + 1 :])
    return jnp.moveaxis(shard.reshape(*before, devices, -1, *after), dim, 0)


def summed_on_arrival(shard, axis, dim):
    blocks = in_blocks(shard, dim, lax.axis_size(axis))
    arrived = lax.all_to_all(blocks, axis, split_axis=0, concat_axis=0, tiled=True)
    return arrived.sum(axis=0)


def from_everyone(shard, axis):
    copies = jnp.broadcast_to(shard, (lax.axis_size(axis), *shard.shape))
    return lax.all_to_all(copies, axis, split_axis=0, concat_axis=0, tiled=True)


def over_copies(shard, axis):
    everything = from_everyone(shard, axis)
    return jnp.sum(everything, axis=0)


def packed_total(arrays, axis):
    ends = [0]
    for a in arrays:
        ends.append(ends[-1] + a.size)
    subtotal = over_copies(jnp.concatenate([a.ravel() for a in arrays]), axis)
    return tuple((subtotal[b:e].reshape(a.shape) for a, b, e in zip(arrays, ends, ends[1:])))


def entropy_term(value):
    return value * jnp.log(jnp.maximum(value, 1.0))


def per_device(counts, labels, edge_tiles, proposals, accept_flags):
    rows_tile = counts.shape[0]
    cols_tile = counts.shape[1]
    row_devices = lax.axis_size("row")
    col_devices = lax.axis_size("col")
    devices = row_devices * col_devices
    edge_count = edge_tiles.shape[0] * edge_tiles.shape[2]
    capacity = 9 * edge_count // (2 * devices)
    first_label = labels[edge_tiles[:, 0, :].reshape(-1)]
    second_label = labels[edge_tiles[:, 1, :].reshape(-1)]
    row_block = jnp.concatenate([first_label, second_label])
    col_block = jnp.concatenate([second_label, first_label])
    entry_count = row_block.shape[0]
    owners = row_block // rows_tile * col_devices + col_block // cols_tile
    owner_match = owners[:, None] == jnp.arange(devices, dtype=jnp.int32)[None, :]
    block_rows = 512
    block_ids = jnp.arange(block_rows, dtype=jnp.int32)
    lower = (block_ids[:, None] >= block_ids[None, :]).astype(jnp.bfloat16)
    stacked_hot = owner_match.astype(jnp.bfloat16).reshape(
        entry_count // block_rows, block_rows, devices
    )
    within = jnp.einsum("ij,bjd->bid", lower, stacked_hot, preferred_element_type=jnp.float32)
    totals = within[:, -1, :]
    earlier = jnp.cumsum(totals, axis=0) - totals
    running = (within + earlier[:, None, :]).reshape(entry_count, devices)
    slot_rank = jnp.sum(jnp.where(owner_match, running, jnp.float32(0.0)), axis=1) - 1.0
    slot_hot = (slot_rank[:, None] == jnp.arange(capacity, dtype=jnp.float32)[None, :]).astype(
        jnp.float32
    )
    row_value = (row_block % rows_tile + 1).astype(jnp.float32)
    col_value = (col_block % cols_tile + 1).astype(jnp.float32)
    carried = jnp.concatenate(
        [slot_hot * row_value[:, None], slot_hot * col_value[:, None]], axis=1
    )
    placed = lax.dot_general(
        owner_match.astype(jnp.float32),
        carried,
        (((0,), (0,)), ((), ())),
        precision=lax.Precision.HIGHEST,
        preferred_element_type=jnp.float32,
    )
    outgoing = placed.reshape(devices, 2, capacity).astype(jnp.int32) - 1
    arrived = lax.all_to_all(outgoing, ("row", "col"), split_axis=0, concat_axis=0, tiled=True)
    per_group = 16
    grouped = arrived.reshape(devices // per_group, per_group, 2, capacity)
    row_ids = jnp.arange(rows_tile, dtype=jnp.int32)
    col_ids = jnp.arange(cols_tile, dtype=jnp.int32)

    def add_group(running_sum, arrived_block):
        wanted_rows = arrived_block[:, 0, :].reshape(-1)
        wanted_cols = arrived_block[:, 1, :].reshape(-1)
        row_hot = (row_ids[:, None] == wanted_rows[None, :]).astype(jnp.bfloat16)
        col_hot = (wanted_cols[:, None] == col_ids[None, :]).astype(jnp.bfloat16)
        return (running_sum + jnp.dot(row_hot, col_hot, preferred_element_type=jnp.float32), None)

    increments, _ = lax.scan(add_group, jnp.zeros((rows_tile, cols_tile), jnp.float32), grouped)
    updated = counts + increments
    col_index = lax.axis_index("col")
    row_index = lax.axis_index("row")
    mine = lax.dynamic_slice_in_dim(proposals, col_index * PROP_COL, PROP_COL, 1)
    source = mine[0]
    target = mine[1]
    own_selector = (source[:, None] == col_index * cols_tile + col_ids[None, :]).astype(jnp.float32)
    own_column = lax.dot_general(
        own_selector,
        updated,
        (((1,), (1,)), ((), ())),
        precision=lax.Precision.HIGHEST,
        preferred_element_type=jnp.float32,
    )
    all_targets = proposals[1]
    selector = (all_targets[:, None] == col_index * cols_tile + col_ids[None, :]).astype(
        jnp.float32
    )
    other_column = summed_on_arrival(
        lax.dot_general(
            selector,
            updated,
            (((1,), (1,)), ((), ())),
            precision=lax.Precision.HIGHEST,
            preferred_element_type=jnp.float32,
        ),
        "col",
        0,
    )
    row_global = row_index * rows_tile + row_ids
    at_source = row_global[None, :] == source[:, None]
    at_target = row_global[None, :] == target[:, None]
    mixed = (
        entropy_term(own_column + other_column)
        - entropy_term(own_column)
        - entropy_term(other_column)
    )
    pair_part = jnp.sum(jnp.where(at_source | at_target, jnp.float32(0.0), mixed), axis=1)
    source_part = jnp.sum(jnp.where(at_source, own_column, jnp.float32(0.0)), axis=1)
    cross_part = jnp.sum(jnp.where(at_source, other_column, jnp.float32(0.0)), axis=1)
    target_part = jnp.sum(jnp.where(at_target, other_column, jnp.float32(0.0)), axis=1)
    degree_part = jnp.sum(own_column, axis=1)
    other_degree = jnp.sum(other_column, axis=1)
    pair_sum, self_source, cross_count, self_target, degree_source, degree_target = packed_total(
        (pair_part, source_part, cross_part, target_part, degree_part, other_degree), "row"
    )
    corner = (
        entropy_term(self_source + 2.0 * cross_count + self_target)
        - entropy_term(self_source)
        - entropy_term(self_target)
        - 2.0 * entropy_term(cross_count)
    )
    change = (
        -(pair_sum + 0.5 * corner)
        + entropy_term(degree_source + degree_target)
        - entropy_term(degree_source)
        - entropy_term(degree_target)
    )
    merge_cost = change / BLOCKS
    accepted_cost = jnp.where(accept_flags == 1, merge_cost, jnp.float32(0.0))
    return (updated, merge_cost, accepted_cost)


def solution(mesh):
    return jax.shard_map(
        per_device,
        mesh=mesh,
        in_specs=(P("row", "col"), P(), P(("row", "col"), None, None), P(), P("col")),
        out_specs=(P("row", "col"), P("col"), P("col")),
        check_vma=False,
    )
```

profile of v0, /device:TPU:1, one launch (start us, length us, event | category | flops | bytes accessed | tf_op | source)
XLA Modules:
  0.0 214.7 jit_solution(8613454886633509514)
XLA Ops:
  0.6 0.9 compare_select_fusion.3
  1.5 52.1 %gather_fusion = s32[4096]{0:T(1024)S(1)} fusion(s32[983040]{0:T(1024)} %param.8, s32[4096]{0:T(1024)S(1)} %broadcast_clamp_fusion.1), kind=kCustom, calls=%fused_computation | custom fusion | bytes 49152 | tf_op jit(solution)/shard_map/gather | solution.py:51
  53.6 52.1 %gather_fusion.1 = s32[4096]{0:T(1024)S(1)} fusion(s32[983040]{0:T(1024)} %param.8, s32[4096]{0:T(1024)S(1)} %broadcast_clamp_fusion), kind=kCustom, calls=%fused_computation.1 | custom fusion | bytes 49152 | tf_op jit(solution)/shard_map/gather | solution.py:52
  105.7 0.1 add_reduce_fusion.1
  105.9 1.3 fusion.14
  107.2 1.9 copy-done.1
  109.2 0.3 slice.62
  109.5 0.3 copy.20
  109.9 0.4 copy.21
  110.2 1.9 subtract_reduce_fusion
  112.1 3.1 %select_reduce_fusion = f32[16,512]{1,0:T(8,128)S(1)} fusion(f32[16,512,128]{1,2,0:T(8,128)} %copy-done.1, f32[16,128]{1,0:T(8,128)S(1)} %subtract_reduce_fusion, s32[16,512]{1,0:T(8,128)S(1)} %fusion.36), kind=kLoop, calls=%fused_computation.20 | loop fusion | flops 4186112 | bytes 4268032 | tf_op jit(solution)/shard_map/reduce_sum | solution.py:68
  115.4 1.1 fusion.12
  116.5 10.3 %fusion.20 = s32[128,288]{0,1:T(8,128)S(1)} fusion(f32[8192,144]{0,1:T(8,128)S(1)} %get-tuple-element.70, f32[8192,144]{0,1:T(8,128)S(1)} %get-tuple-element.69, s32[8192]{0:T(1024)S(1)} %get-tuple-element.66), kind=kOutput, calls=%fused_computation.28 | convolution fusion | flops 3627360256 | bytes 9617408 | tf_op jit(solution)/shard_map/dot_general | solution.py:77
  126.8 0.8 copy.22
  127.6 11.5 %all-to-all-start = ((s32[128,2,144]{2,1,0:T(2,128)}), s32[128,2,144]{2,1,0:T(2,128)S(1)}, u32[]{:S(2)}, u32[]{:S(2)}) async-start(s32[128,2,144]{2,1,0:T(2,128)} %copy.22), calls=%async_computation | async-start | bytes 524288 | tf_op jit(solution)/shard_map/all_to_all | solution.py:85
  139.2 11.4 %all-to-all-done = s32[128,2,144]{2,1,0:T(2,128)S(1)} async-done(((s32[128,2,144]{2,1,0:T(2,128)}), s32[128,2,144]{2,1,0:T(2,128)S(1)}, u32[]{:S(2)}, u32[]{:S(2)}) %all-to-all-start) | async-done | bytes 147488 | tf_op jit(solution)/shard_map/all_to_all | solution.py:85
  150.5 26.6 %while.11 = (s32[]{:T(128)}, f32[1024,512]{1,0:T(8,128)S(1)}, s32[8,16,2,144]{3,2,1,0:T(2,128)S(1)}, s32[]{:T(128)}, s32[]{:T(128)}) while((s32[]{:T(128)}, f32[1024,512]{1,0:T(8,128)S(1)}, s32[8,16,2,144]{3,2,1,0:T(2,128)S(1)}, s32[]{:T(128)}, s32[]{:T(128)}) %tuple.45), condition=%wide.region_3.4_spmd.clone, body=%wide.region_2.3_spmd.clone.sunk | while | flops 2420506624 | bytes 4323403 | solution.py:98
  150.5 0.1 slice_reduce_fusion.3
  150.6 0.1 eq.288
  150.7 0.1 eq.289
  150.8 3.0 %select_add_fusion.2 = f32[1024,512]{1,0:T(8,128)S(1)} fusion(f32[1024,512]{1,0:T(8,128)S(1)} %get-tuple-element.106, s32[2304]{0:T(1024)S(1)} %eq.288, s32[2304]{0:T(1024)S(1)} %eq.289, pred[]{:T(512)S(6)} %compare.27), kind=kOutput, calls=%fused_computation.9.clone.1 | convolution fusion | flops 2420506624 | bytes 4212737 | tf_op jit(solution)/shard_map/while/body/eval_jaxpr/dot_general | solution.py:96
  153.9 0.1 slice_reduce_fusion.3
  154.0 0.1 eq.288
  154.0 0.1 eq.289
  154.1 3.0 %select_add_fusion.2 = f32[1024,512]{1,0:T(8,128)S(1)} fusion(f32[1024,512]{1,0:T(8,128)S(1)} %get-tuple-element.106, s32[2304]{0:T(1024)S(1)} %eq.288, s32[2304]{0:T(1024)S(1)} %eq.289, pred[]{:T(512)S(6)} %compare.27), kind=kOutput, calls=%fused_computation.9.clone.1 | convolution fusion | flops 2420506624 | bytes 4212737 | tf_op jit(solution)/shard_map/while/body/eval_jaxpr/dot_general | solution.py:96
  157.2 0.1 slice_reduce_fusion.3
  157.3 0.1 eq.288
  157.5 3.0 %select_add_fusion.2 = f32[1024,512]{1,0:T(8,128)S(1)} fusion(f32[1024,512]{1,0:T(8,128)S(1)} %get-tuple-element.106, s32[2304]{0:T(1024)S(1)} %eq.288, s32[2304]{0:T(1024)S(1)} %eq.289, pred[]{:T(512)S(6)} %compare.27), kind=kOutput, calls=%fused_computation.9.clone.1 | convolution fusion | flops 2420506624 | bytes 4212737 | tf_op jit(solution)/shard_map/while/body/eval_jaxpr/dot_general | solution.py:96
  160.5 0.1 slice_reduce_fusion.3
  160.8 3.0 %select_add_fusion.2 = f32[1024,512]{1,0:T(8,128)S(1)} fusion(f32[1024,512]{1,0:T(8,128)S(1)} %get-tuple-element.106, s32[2304]{0:T(1024)S(1)} %eq.288, s32[2304]{0:T(1024)S(1)} %eq.289, pred[]{:T(512)S(6)} %compare.27), kind=kOutput, calls=%fused_computation.9.clone.1 | convolution fusion | flops 2420506624 | bytes 4212737 | tf_op jit(solution)/shard_map/while/body/eval_jaxpr/dot_general | solution.py:96
  163.9 0.1 slice_reduce_fusion.3
  164.1 3.0 %select_add_fusion.2 = f32[1024,512]{1,0:T(8,128)S(1)} fusion(f32[1024,512]{1,0:T(8,128)S(1)} %get-tuple-element.106, s32[2304]{0:T(1024)S(1)} %eq.288, s32[2304]{0:T(1024)S(1)} %eq.289, pred[]{:T(512)S(6)} %compare.27), kind=kOutput, calls=%fused_computation.9.clone.1 | convolution fusion | flops 2420506624 | bytes 4212737 | tf_op jit(solution)/shard_map/while/body/eval_jaxpr/dot_general | solution.py:96
  167.2 0.1 slice_reduce_fusion.3
  167.5 3.0 %select_add_fusion.2 = f32[1024,512]{1,0:T(8,128)S(1)} fusion(f32[1024,512]{1,0:T(8,128)S(1)} %get-tuple-element.106, s32[2304]{0:T(1024)S(1)} %eq.288, s32[2304]{0:T(1024)S(1)} %eq.289, pred[]{:T(512)S(6)} %compare.27), kind=kOutput, calls=%fused_computation.9.clone.1 | convolution fusion | flops 2420506624 | bytes 4212737 | tf_op jit(solution)/shard_map/while/body/eval_jaxpr/dot_general | solution.py:96
  170.5 0.1 slice_reduce_fusion.3
  170.8 3.0 %select_add_fusion.2 = f32[1024,512]{1,0:T(8,128)S(1)} fusion(f32[1024,512]{1,0:T(8,128)S(1)} %get-tuple-element.106, s32[2304]{0:T(1024)S(1)} %eq.288, s32[2304]{0:T(1024)S(1)} %eq.289, pred[]{:T(512)S(6)} %compare.27), kind=kOutput, calls=%fused_computation.9.clone.1 | convolution fusion | flops 2420506624 | bytes 4212737 | tf_op jit(solution)/shard_map/while/body/eval_jaxpr/dot_general | solution.py:96
  173.9 0.1 slice_reduce_fusion.3
  174.1 3.0 %select_add_fusion.2 = f32[1024,512]{1,0:T(8,128)S(1)} fusion(f32[1024,512]{1,0:T(8,128)S(1)} %get-tuple-element.106, s32[2304]{0:T(1024)S(1)} %eq.288, s32[2304]{0:T(1024)S(1)} %eq.289, pred[]{:T(512)S(6)} %compare.27), kind=kOutput, calls=%fused_computation.9.clone.1 | convolution fusion | flops 2420506624 | bytes 4212737 | tf_op jit(solution)/shard_map/while/body/eval_jaxpr/dot_general | solution.py:96
  177.2 1.3 copy-done.2
  178.5 2.7 %add.156 = f32[1024,512]{1,0:T(8,128)S(1)} add(f32[1024,512]{1,0:T(8,128)} %param.7, f32[1024,512]{1,0:T(8,128)} %copy-done.2) | non-fusion elementwise | flops 524288 | bytes 6291456 | tf_op jit(solution)/shard_map/add | solution.py:99
  181.2 2.3 %fusion.25 = f32[256,1024]{1,0:T(8,128)} fusion(f32[1024,512]{1,0:T(8,128)S(1)} %add.156, s32[512]{0:T(512)S(1)} %iota_add_fusion.1, s32[256]{0:T(256)S(1)} %bitcast.40), kind=kOutput, calls=%fused_computation.32 | convolution fusion | flops 1610743808 | bytes 3148800 | tf_op jit(solution)/shard_map/dot_general | solution.py:118
  183.5 3.7 %all-to-all-start.1 = ((f32[16,16,1024]{2,1,0:T(8,128)}), f32[16,16,1024]{2,1,0:T(8,128)S(1)}, u32[]{:S(2)}, u32[]{:S(2)}) async-start(f32[16,16,1024]{2,1,0:T(8,128)} %bitcast.13), calls=%async_computation.1 | async-start | bytes 2097152 | tf_op jit(solution)/shard_map/all_to_all | solution.py:17
  187.2 16.4 %all-to-all-done.1 = f32[16,16,1024]{2,1,0:T(8,128)S(1)} async-done(((f32[16,16,1024]{2,1,0:T(8,128)}), f32[16,16,1024]{2,1,0:T(8,128)S(1)}, u32[]{:S(2)}, u32[]{:S(2)}) %all-to-all-start.1) | async-done | bytes 1048608 | tf_op jit(solution)/shard_map/all_to_all | solution.py:17
  203.6 0.2 fusion.53
  203.8 1.2 fusion.29
  205.1 0.1 concatenate.79
  205.2 8.9 %all_to_all.16 = f32[8,1,96]{2,1,0:T(1,128)S(1)} all-to-all(f32[8,1,96]{2,1,0:T(1,128)S(1)} %broadcast_in_dim.22), channel_id=1, replica_groups=mesh['row'=8,'col'=16] {'row'}, dimensions={0} | all-to-all | bytes 6144 | tf_op jit(solution)/shard_map/all_to_all | solution.py:23
  214.1 0.6 compare_select_fusion.5
  (47 shorter events, 1.3 us)
Async XLA Ops:
  107.2 1.9 copy-start.1
  116.5 22.6 %copy-start.3 = (s32[2,256]{1,0:T(2,128)S(1)}, s32[2,256]{1,0:T(2,128)}, u32[]{:S(2)}) copy-start(s32[2,256]{1,0:T(2,128)} %param.10) | copy-start | bytes 6148
  127.6 22.9 %all-to-all-start = ((s32[128,2,144]{2,1,0:T(2,128)}), s32[128,2,144]{2,1,0:T(2,128)S(1)}, u32[]{:S(2)}, u32[]{:S(2)}) async-start(s32[128,2,144]{2,1,0:T(2,128)} %copy.22), calls=%async_computation | async-start | bytes 524288 | tf_op jit(solution)/shard_map/all_to_all | solution.py:85
  177.2 1.3 copy-start.2
  181.2 23.9 %copy-start = (f32[1024,512]{1,0:T(8,128)}, f32[1024,512]{1,0:T(8,128)S(1)}, u32[]{:S(2)}) copy-start(f32[1024,512]{1,0:T(8,128)S(1)} %add.156) | copy-start | bytes 6291460
  181.2 32.9 %copy-start.4 = (s32[16]{0:T(128)S(1)}, s32[16]{0:T(128)}, u32[]{:S(2)}) copy-start(s32[16]{0:T(128)} %param.11) | copy-start | bytes 196
  183.5 20.1 %all-to-all-start.1 = ((f32[16,16,1024]{2,1,0:T(8,128)}), f32[16,16,1024]{2,1,0:T(8,128)S(1)}, u32[]{:S(2)}, u32[]{:S(2)}) async-start(f32[16,16,1024]{2,1,0:T(8,128)} %bitcast.13), calls=%async_computation.1 | async-start | bytes 2097152 | tf_op jit(solution)/shard_map/all_to_all | solution.py:17
where the time goes:
time: 219 us; the launch traced here: 215 us
  local copies, waits for them, and re-layouts  112 us (51%)
  matrix products  39.3 us (18%)
  waiting for transfers between devices  27.7 us (13%)
  starting transfers between devices  15.1 us (7%)
  other arithmetic  10.8 us (5%)
  blocking collectives  8.87 us (4%)
    gather x1, local copies, waits for them, and re-layouts, per_device(): first_label = labels[edge_tiles[:, 0, :].reshape(-1)]  52.1 us
    gather x1, local copies, waits for them, and re-layouts, per_device(): second_label = labels[edge_tiles[:, 1, :].reshape(-1)]  52.1 us
    dot_general x8, matrix products, add_group(): jnp.dot(row_hot, col_hot, preferred_element_type=jnp.float32)  24.2 us
    all_to_all x1, waiting for transfers between devices, summed_on_arrival(): lax.all_to_all(blocks, axis, split_axis=0, concat_axis=0, tiled=True)  16.4 us
    all_to_all x1, starting transfers between devices, per_device(): lax.all_to_all(outgoing, ('row', 'col'), split_axis=0, concat_axis=0, til...  11.5 us
    all_to_all x1, waiting for transfers between devices, per_device(): lax.all_to_all(outgoing, ('row', 'col'), split_axis=0, concat_axis=0, til...  11.4 us
    dot_general x1, matrix products, per_device(): lax.dot_general(owner_match.astype(jnp.float32), carried, (((0,), (0,)),...  10.3 us
    all_to_all x1, blocking collectives, from_everyone(): return lax.all_to_all(copies, axis, split_axis=0, concat_axis=0, tiled=True)  8.87 us
  transfers between devices with their start and end apart: 2, of which 2 were waited for; matrix products, arithmetic and copies ran while one was open for 0% of the time, Pallas kernels for 0%

commit v1 on v0

--- a/solution.py
+++ b/solution.py
@@ -1,10 +1,132 @@
+import functools
+
 import jax
 import jax.numpy as jnp
 from jax import lax
+from jax.experimental import pallas as pl
+from jax.experimental.pallas import tpu as pltpu
 from jax.sharding import PartitionSpec as P
 
+I32 = jnp.int32
+F32 = jnp.float32
+BF = jnp.bfloat16
+F8 = jnp.float8_e4m3fn
+LANES = 128
 BLOCKS = 8192
 PROP_COL = 16
+MESH = pl.DeviceIdType.MESH
+
+
+def start_gather(evm, hi, sms, sem):
+    hi[...] = lax.shift_right_logical(evm[...], 7)
+    for k in range(len(sms)):
+        pltpu.make_async_copy(hi.at[k], sms[k], sem.at[k]).start()
+
+
+def gather_labels(evm, table, lab, hi, sms, g, sem):
+    tiles = evm.shape[0]
+    depth = len(sms)
+    sub = lax.broadcasted_iota(I32, (LANES, LANES), 0)
+
+    def finish(t, slot):
+        for side in (0, 1):
+            lanes = evm[t, pl.ds(side, 1), :] & (LANES - 1)
+            picked = jnp.where(sub == lanes, g[slot, side].T, 0)
+            lab[pl.ds(side, 1), pl.ds(pl.multiple_of(t * LANES, LANES), LANES)] = jnp.sum(
+                picked, axis=0, keepdims=True
+            )
+
+    def body(u, _):
+        for k in range(depth):
+            t = depth * u + k
+            pltpu.make_async_copy(hi.at[t], sms[k], sem.at[k]).wait()
+            finish(jnp.maximum(t - 1, 0), (k + 1) % 2)
+            for side in (0, 1):
+                for e in range(LANES):
+                    g[k % 2, side, pl.ds(e, 1), :] = table[pl.ds(sms[k][side, e], 1), :]
+            later = jnp.minimum(t + depth, tiles - 1)
+            pltpu.make_async_copy(hi.at[later], sms[k], sem.at[k]).start()
+        return 0
+
+    lax.fori_loop(0, tiles // depth, body, 0)
+    for k in range(depth):
+        pltpu.make_async_copy(hi.at[tiles - 1], sms[k], sem.at[k]).wait()
+    finish(tiles - 1, (depth - 1) % 2)
+
+
+BLOCK = 256
+GROUP = 4
+
+
+def place_entries(lab, send, acc, rows_tile, cols_tile, col_devices):
+    edges = lab.shape[1]
+    wide = GROUP * BLOCK
+    upper = (
+        lax.broadcasted_iota(I32, (BLOCK, BLOCK), 0) <= lax.broadcasted_iota(I32, (BLOCK, BLOCK), 1)
+    ).astype(F32).astype(BF)
+    dev = lax.broadcasted_iota(I32, (LANES, BLOCK), 0)
+    dev16 = dev.astype(F32).astype(BF)
+    one = jnp.ones((LANES, BLOCK), BF)
+    zero = jnp.zeros((LANES, BLOCK), BF)
+    tail_id = lax.broadcasted_iota(I32, (16, BLOCK), 0) + LANES
+    tail16 = tail_id.astype(F32).astype(BF)
+    tail_zero = jnp.zeros((16, BLOCK), BF)
+    acc[...] = jnp.zeros_like(acc)
+
+    def cast(x):
+        return x.astype(F32).astype(BF)
+
+    def group(side):
+        def body(u, base):
+            lanes = pl.ds(pl.multiple_of(u * wide, wide), wide)
+            rlab = lab[pl.ds(side, 1), lanes]
+            clab = lab[pl.ds(1 - side, 1), lanes]
+            owner = (rlab // rows_tile) * col_devices + clab // cols_tile
+            row = rlab % rows_tile + 1
+            col = clab % cols_tile
+            owner16 = cast(owner)
+            pieces = [cast(row >> 5), cast(col >> 5), cast(row & 31), cast(col & 31)]
+            hots = []
+            for q in range(GROUP):
+                cut = slice(q * BLOCK, (q + 1) * BLOCK)
+                hots.append(
+                    jnp.where(dev16 == jnp.broadcast_to(owner16[:, cut], dev.shape), one, zero)
+                )
+            within = jnp.dot(jnp.concatenate(hots, 0), upper, preferred_element_type=F32)
+            total = jnp.zeros((LANES, 288), F32)
+            for q in range(GROUP):
+                cut = slice(q * BLOCK, (q + 1) * BLOCK)
+                w = within[q * LANES : (q + 1) * LANES]
+                running = w + jnp.concatenate([base, base], 1)
+                slot = jnp.sum(hots[q].astype(F32) * running, axis=0, keepdims=True) - 1.0
+                base = base + jnp.broadcast_to(w[:, BLOCK - 1 :], base.shape)
+                slot16 = slot.astype(BF)
+                main = dev16 == jnp.broadcast_to(slot16, dev.shape)
+                tail = tail16 == jnp.broadcast_to(slot16, tail_id.shape)
+
+                def spread(v):
+                    v = v[:, cut]
+                    return (
+                        jnp.where(main, jnp.broadcast_to(v, dev.shape), zero),
+                        jnp.where(tail, jnp.broadcast_to(v, tail_id.shape), tail_zero),
+                    )
+
+                rh, ch, rl, cl = [spread(v) for v in pieces]
+                high = jnp.concatenate([rh[0], ch[0], rh[1], ch[1]], 0)
+                low = jnp.concatenate([rl[0], cl[0], rl[1], cl[1]], 0)
+                nt = (((1,), (1,)), ((), ()))
+                total += lax.dot_general(hots[q] * 32.0, high, nt, preferred_element_type=F32)
+                total += lax.dot_general(hots[q], low, nt, preferred_element_type=F32)
+            acc[:, :288] += total
+            return base
+
+        return body
+
+    base = jnp.zeros((LANES, LANES), F32)
+    for side in (0, 1):
+        base = lax.fori_loop(0, edges // wide, group(side), base)
+    for k in range(3):
+        send[k] = acc[:, k * LANES : (k + 1) * LANES].astype(I32)
 
 
 def in_blocks(shard, dim, devices):
@@ -40,63 +162,125 @@
     return value * jnp.log(jnp.maximum(value, 1.0))
 
 
+def exchange_kernel(row_n, col_n, evm, table, out, lab, hi, s0, s1, s2, s3, g, send, recv, acc, sem, ssem, rsem):
+    devices = row_n * col_n
+    me = lax.axis_index("row") * col_n + lax.axis_index("col")
+    sms = (s0, s1, s2, s3)
+    barrier = pltpu.get_barrier_semaphore()
+
+    def greet(k, _):
+        d = lax.rem(me + k, devices)
+        pl.semaphore_signal(barrier, inc=1, device_id=(d // col_n, lax.rem(d, col_n)), device_id_type=MESH)
+        return 0
+
+    lax.fori_loop(1, devices, greet, 0)
+    start_gather(evm, hi, sms, sem)
+    gather_labels(evm, table, lab, hi, sms, g, sem)
+    place_entries(lab, send, acc, BLOCKS // row_n, BLOCKS // col_n, col_n)
+    pl.semaphore_wait(barrier, devices - 1)
+
+    def push(k, _):
+        d = lax.rem(me + k, devices)
+        pltpu.make_async_remote_copy(
+            src_ref=send.at[:, pl.ds(d, 1), :],
+            dst_ref=recv.at[:, pl.ds(me, 1), :],
+            send_sem=ssem,
+            recv_sem=rsem,
+            device_id=(d // col_n, lax.rem(d, col_n)),
+            device_id_type=MESH,
+        ).start()
+        return 0
+
+    lax.fori_loop(1, devices, push, 0)
+    rest = pl.ds(0, devices - 1)
+    pltpu.make_async_copy(recv.at[:, rest, :], recv.at[:, rest, :], rsem).wait()
+    pltpu.make_async_copy(send.at[:, rest, :], send.at[:, rest, :], ssem).wait()
+    own = send[:, pl.ds(me, 1), :]
+    recv[:, pl.ds(me, 1), :] = own
+    tails = recv[2].T
+    out[0, :LANES, :] = recv[0] - 1
+    out[1, :LANES, :] = recv[1]
+    out[0, LANES:, :] = tails[:16] - 1
+    out[1, LANES:, :] = tails[16:32]
+
+
+def exchange(edge_tiles, labels, row_n, col_n):
+    small = pltpu.SMEM((2, LANES), I32)
+    return pl.pallas_call(
+        functools.partial(exchange_kernel, row_n, col_n),
+        out_shape=jax.ShapeDtypeStruct((2, LANES + 16, LANES), I32),
+        in_specs=[pl.BlockSpec(memory_space=pltpu.VMEM)] * 2,
+        out_specs=pl.BlockSpec(memory_space=pltpu.VMEM),
+        scratch_shapes=[
+            pltpu.VMEM((2, 4096), I32),
+            pltpu.VMEM((32, 2, LANES), I32),
+            small,
+            small,
+            small,
+            small,
+            pltpu.VMEM((2, 2, LANES, LANES), I32),
+            pltpu.VMEM((3, LANES, LANES), I32),
+            pltpu.VMEM((3, LANES, LANES), I32),
+            pltpu.VMEM((LANES, 384), F32),
+            pltpu.SemaphoreType.DMA((4,)),
+            pltpu.SemaphoreType.DMA,
+            pltpu.SemaphoreType.DMA,
+        ],
+        compiler_params=pltpu.CompilerParams(collective_id=0, has_side_effects=True),
+    )(edge_tiles, labels.reshape(-1, LANES))
+
+
+def one_hot(v, n):
+    wide = v.shape[1]
+    ids = lax.broadcasted_iota(I32, (256, wide), 0).astype(F32).astype(BF)
+    one = jnp.ones((256, wide), BF)
+    zero = jnp.zeros((256, wide), BF)
+    out = []
+    for b in range(n // 256):
+        w = jnp.where((v >> 8) == b, v & 255, -1).astype(F32).astype(BF)
+        out.append(jnp.where(ids == jnp.broadcast_to(w, ids.shape), one, zero).astype(F8))
+    return jnp.concatenate(out, 0)
+
+
+STEP = 16
+
+
+def add_kernel(entries, counts, out):
+    out[...] = counts[...]
+
+    def body(i, _):
+        r = jnp.concatenate([entries[0, pl.ds(i * STEP + q, 1), :] for q in range(STEP)], 1)
+        c = jnp.concatenate([entries[1, pl.ds(i * STEP + q, 1), :] for q in range(STEP)], 1)
+        out[...] += lax.dot_general(
+            one_hot(r, out.shape[0]),
+            one_hot(c, out.shape[1]),
+            (((1,), (1,)), ((), ())),
+            preferred_element_type=F32,
+        )
+        return 0
+
+    lax.fori_loop(0, entries.shape[1] // STEP, body, 0)
+
+
+def add_entries(entries, counts):
+    return pl.pallas_call(
+        add_kernel,
+        out_shape=jax.ShapeDtypeStruct(counts.shape, F32),
+        in_specs=[pl.BlockSpec(memory_space=pltpu.VMEM)] * 2,
+        out_specs=pl.BlockSpec(memory_space=pltpu.VMEM),
+        compiler_params=pltpu.CompilerParams(vmem_limit_bytes=60 << 20),
+    )(entries, counts)
+
+
 def per_device(counts, labels, edge_tiles, proposals, accept_flags):
     rows_tile = counts.shape[0]
     cols_tile = counts.shape[1]
     row_devices = lax.axis_size("row")
     col_devices = lax.axis_size("col")
-    devices = row_devices * col_devices
-    edge_count = edge_tiles.shape[0] * edge_tiles.shape[2]
-    capacity = 9 * edge_count // (2 * devices)
-    first_label = labels[edge_tiles[:, 0, :].reshape(-1)]
-    second_label = labels[edge_tiles[:, 1, :].reshape(-1)]
-    row_block = jnp.concatenate([first_label, second_label])
-    col_block = jnp.concatenate([second_label, first_label])
-    entry_count = row_block.shape[0]
-    owners = row_block // rows_tile * col_devices + col_block // cols_tile
-    owner_match = owners[:, None] == jnp.arange(devices, dtype=jnp.int32)[None, :]
-    block_rows = 512
-    block_ids = jnp.arange(block_rows, dtype=jnp.int32)
-    lower = (block_ids[:, None] >= block_ids[None, :]).astype(jnp.bfloat16)
-    stacked_hot = owner_match.astype(jnp.bfloat16).reshape(
-        entry_count // block_rows, block_rows, devices
-    )
-    within = jnp.einsum("ij,bjd->bid", lower, stacked_hot, preferred_element_type=jnp.float32)
-    totals = within[:, -1, :]
-    earlier = jnp.cumsum(totals, axis=0) - totals
-    running = (within + earlier[:, None, :]).reshape(entry_count, devices)
-    slot_rank = jnp.sum(jnp.where(owner_match, running, jnp.float32(0.0)), axis=1) - 1.0
-    slot_hot = (slot_rank[:, None] == jnp.arange(capacity, dtype=jnp.float32)[None, :]).astype(
-        jnp.float32
-    )
-    row_value = (row_block % rows_tile + 1).astype(jnp.float32)
-    col_value = (col_block % cols_tile + 1).astype(jnp.float32)
-    carried = jnp.concatenate(
-        [slot_hot * row_value[:, None], slot_hot * col_value[:, None]], axis=1
-    )
-    placed = lax.dot_general(
-        owner_match.astype(jnp.float32),
-        carried,
-        (((0,), (0,)), ((), ())),
-        precision=lax.Precision.HIGHEST,
-        preferred_element_type=jnp.float32,
-    )
-    outgoing = placed.reshape(devices, 2, capacity).astype(jnp.int32) - 1
-    arrived = lax.all_to_all(outgoing, ("row", "col"), split_axis=0, concat_axis=0, tiled=True)
-    per_group = 16
-    grouped = arrived.reshape(devices // per_group, per_group, 2, capacity)
     row_ids = jnp.arange(rows_tile, dtype=jnp.int32)
     col_ids = jnp.arange(cols_tile, dtype=jnp.int32)
-
-    def add_group(running_sum, arrived_block):
-        wanted_rows = arrived_block[:, 0, :].reshape(-1)
-        wanted_cols = arrived_block[:, 1, :].reshape(-1)
-        row_hot = (row_ids[:, None] == wanted_rows[None, :]).astype(jnp.bfloat16)
-        col_hot = (wanted_cols[:, None] == col_ids[None, :]).astype(jnp.bfloat16)
-        return (running_sum + jnp.dot(row_hot, col_hot, preferred_element_type=jnp.float32), None)
-
-    increments, _ = lax.scan(add_group, jnp.zeros((rows_tile, cols_tile), jnp.float32), grouped)
-    updated = counts + increments
+    entries = exchange(edge_tiles, labels, row_devices, col_devices)
+    updated = add_entries(entries, counts)
     col_index = lax.axis_index("col")
     row_index = lax.axis_index("row")
     mine = lax.dynamic_slice_in_dim(proposals, col_index * PROP_COL, PROP_COL, 1)

time: 219 us -> 83.6 us (0.38); the launches traced: 215 us -> 83.3 us
  local copies, waits for them, and re-layouts: 112 us -> 0.87 us
  Pallas kernels: 0 us -> 46.2 us
  matrix products: 39.3 us -> 5.07 us
  starting transfers between devices: 15.1 us -> 3.78 us
  waiting for transfers between devices: 27.7 us -> 16.4 us
  other arithmetic: 10.8 us -> 0.88 us
    gather x2 -> x0, local copies, waits for them, and re-layouts: 104 us -> none  [the longest x1 52.1 us: per_device(): first_label = labels[edge_tiles[:, 0, :].reshape(-1)]]
    pallas_call x0 -> x2, Pallas kernels: none -> 46.2 us  [the longest x1 32 us: exchange(): pl.pallas_call(functools.partial(exchange_kernel, row_n, col_n), out_shap...]
    dot_general x10 -> x0, matrix products: 35.8 us -> none  [the longest x8 24.2 us: add_group(): jnp.dot(row_hot, col_hot, preferred_element_type=jnp.float32)]
    all_to_all x1 -> x0, starting transfers between devices: 11.5 us -> none  [per_device(): lax.all_to_all(outgoing, ('row', 'col'), split_axis=0, concat_axis=0, til...]
    all_to_all x1 -> x0, waiting for transfers between devices: 11.4 us -> none  [per_device(): lax.all_to_all(outgoing, ('row', 'col'), split_axis=0, concat_axis=0, til...]
    unnamed x12 -> x6, local copies, waits for them, and re-layouts: 3.26 us -> 0.01 us
    reduce_sum x1 -> x0, other arithmetic: 3.13 us -> none  [per_device(): jnp.sum(jnp.where(owner_match, running, jnp.float32(0.0)), axis=1) - 1.0]
    add x3 -> x0, other arithmetic: 2.81 us -> none  [the longest x1 2.7 us: per_device(): updated = counts + increments]
  transfers between devices with their start and end apart: 2 -> 1, of which waited for: 2 -> 1; matrix products, arithmetic and copies ran while one was open for 0% -> 0% of each run, Pallas kernels for 0% -> 0%
where the time goes in v1:
time: 83.6 us; the launch traced here: 83.3 us
  Pallas kernels  46.2 us (55%)
  waiting for transfers between devices  16.4 us (20%)
  blocking collectives  9.38 us (11%)
  matrix products  5.07 us (6%)
  starting transfers between devices  3.78 us (5%)
  other arithmetic  0.88 us (1%)
  local copies, waits for them, and re-layouts  0.87 us (1%)
    pallas_call x1, Pallas kernels, exchange(): pl.pallas_call(functools.partial(exchange_kernel, row_n, col_n), out_shap...  32 us
    all_to_all x1, waiting for transfers between devices, summed_on_arrival(): lax.all_to_all(blocks, axis, split_axis=0, concat_axis=0, tiled=True)  16.4 us
    pallas_call x1, Pallas kernels, add_entries(): pl.pallas_call(add_kernel, out_shape=jax.ShapeDtypeStruct(counts.shape, F...  14.2 us
    all_to_all x1, blocking collectives, from_everyone(): return lax.all_to_all(copies, axis, split_axis=0, concat_axis=0, tiled=True)  9.38 us
    dot_general x1, matrix products, per_device(): lax.dot_general(selector, updated, (((1,), (1,)), ((), ())), precision=la...  3.84 us
    all_to_all x1, starting transfers between devices, summed_on_arrival(): lax.all_to_all(blocks, axis, split_axis=0, concat_axis=0, tiled=True)  3.78 us
  transfers between devices with their start and end apart: 1, of which 1 were waited for; matrix products, arithmetic and copies ran while one was open for 0% of the time, Pallas kernels for 0%

profile of v1, /device:TPU:1, one launch (start us, length us, event | category | flops | bytes accessed | tf_op | source)
XLA Modules:
  0.0 83.3 jit_solution(4602979360322600324)
XLA Ops:
  0.6 0.7 slice.29
  1.3 32.0 %shard_map.76.entries = s32[2,144,128]{2,1,0:T(8,128)} custom-call(s32[32,2,128]{2,1,0:T(2,128)} %evm.1, s32[7680,128]{1,0:T(8,128)} %bitcast.10), custom_call_target="tpu_custom_call" | custom-call | tf_op jit(solution)/shard_map/pallas_call | solution.py:209
  33.3 14.2 %shard_map.77 = f32[1024,512]{1,0:T(8,128)} custom-call(s32[2,144,128]{2,1,0:T(8,128)} %shard_map.76.entries, f32[1024,512]{1,0:T(8,128)} %counts.1), custom_call_target="tpu_custom_call" | custom-call | tf_op jit(solution)/shard_map/pallas_call | solution.py:266
  47.6 0.0 copy-start.1
  47.6 3.8 %fusion = f32[256,1024]{1,0:T(8,128)} fusion(f32[1024,512]{1,0:T(8,128)} %shard_map.77, s32[512]{0:T(512)S(1)} %iota_add_fusion.1, s32[256]{0:T(256)S(1)} %bitcast.12), kind=kOutput, calls=%fused_computation | convolution fusion | flops 1610743808 | bytes 3148800 | tf_op jit(solution)/shard_map/dot_general | solution.py:302
  51.4 0.0 copy-start
  51.4 3.8 %all-to-all-start = ((f32[16,16,1024]{2,1,0:T(8,128)}), f32[16,16,1024]{2,1,0:T(8,128)S(1)}, u32[]{:S(2)}, u32[]{:S(2)}) async-start(f32[16,16,1024]{2,1,0:T(8,128)} %bitcast.4), calls=%async_computation | async-start | bytes 2097152 | tf_op jit(solution)/shard_map/all_to_all | solution.py:139
  55.2 0.0 copy-start.2
  55.2 0.0 copy-done.1
  55.2 0.1 constant_dynamic-slice_fusion
  55.3 16.4 %all-to-all-done = f32[16,16,1024]{2,1,0:T(8,128)S(1)} async-done(((f32[16,16,1024]{2,1,0:T(8,128)}), f32[16,16,1024]{2,1,0:T(8,128)S(1)}, u32[]{:S(2)}, u32[]{:S(2)}) %all-to-all-start) | async-done | bytes 1048608 | tf_op jit(solution)/shard_map/all_to_all | solution.py:139
  71.7 0.2 fusion.11
  71.9 0.0 copy-done
  71.9 1.2 %fusion.4 = (f32[16]{0:T(128)S(1)}, f32[16]{0:T(128)S(1)}, f32[16]{0:T(128)S(1)}, f32[16]{0:T(128)S(1)}, f32[16]{0:T(128)S(1)}) fusion(f32[16,1024]{1,0:T(8,128)S(1)} %get-tuple-element.4, s32[1024]{0:T(1024)S(1)} %iota_add_fusion, s32[16]{0:T(128)S(1)} %get-tuple-element.13, s32[16]{0:T(128)S(1)} %get-tuple-element.12, f32[1024,512]{1,0:T(8,128)S(1)} %copy-done, ...), kind=kOutput, calls=%fused_computation.8 | convolution fusion | flops 101015472 | bytes 2169280 | tf_op jit(solution)/shard_map/dot_general | solution.py:290
  73.2 0.1 concatenate.3
  73.2 9.4 %all_to_all.11 = f32[8,1,96]{2,1,0:T(1,128)S(1)} all-to-all(f32[8,1,96]{2,1,0:T(1,128)S(1)} %broadcast_in_dim.20), channel_id=1, replica_groups=mesh['row'=8,'col'=16] {'row'}, dimensions={0} | all-to-all | bytes 6144 | tf_op jit(solution)/shard_map/all_to_all | solution.py:145
  82.6 0.0 copy-done.2
  82.6 0.6 compare_select_fusion.3
  (5 shorter events, 0.0 us)
Async XLA Ops:
  47.6 7.7 %copy-start.1 = (s32[2,256]{1,0:T(2,128)S(1)}, s32[2,256]{1,0:T(2,128)}, u32[]{:S(2)}) copy-start(s32[2,256]{1,0:T(2,128)} %param.8) | copy-start | bytes 6148
  51.4 20.5 %copy-start = (f32[1024,512]{1,0:T(8,128)S(1)}, f32[1024,512]{1,0:T(8,128)}, u32[]{:S(2)}) copy-start(f32[1024,512]{1,0:T(8,128)} %shard_map.77) | copy-start | bytes 6291460
  51.4 20.3 %all-to-all-start = ((f32[16,16,1024]{2,1,0:T(8,128)}), f32[16,16,1024]{2,1,0:T(8,128)S(1)}, u32[]{:S(2)}, u32[]{:S(2)}) async-start(f32[16,16,1024]{2,1,0:T(8,128)} %bitcast.4), calls=%async_computation | async-start | bytes 2097152 | tf_op jit(solution)/shard_map/all_to_all | solution.py:139
  55.2 27.5 %copy-start.2 = (s32[16]{0:T(128)S(1)}, s32[16]{0:T(128)}, u32[]{:S(2)}) copy-start(s32[16]{0:T(128)} %param.9) | copy-start | bytes 196

commit v2 on v1

--- a/solution.py
+++ b/solution.py
@@ -13,7 +13,6 @@
 F8 = jnp.float8_e4m3fn
 LANES = 128
 BLOCKS = 8192
-PROP_COL = 16
 MESH = pl.DeviceIdType.MESH
 
 
@@ -129,39 +128,6 @@
         send[k] = acc[:, k * LANES : (k + 1) * LANES].astype(I32)
 
 
-def in_blocks(shard, dim, devices):
-    before, after = (shard.shape[:dim], shard.shape[dim + 1 :])
-    return jnp.moveaxis(shard.reshape(*before, devices, -1, *after), dim, 0)
-
-
-def summed_on_arrival(shard, axis, dim):
-    blocks = in_blocks(shard, dim, lax.axis_size(axis))
-    arrived = lax.all_to_all(blocks, axis, split_axis=0, concat_axis=0, tiled=True)
-    return arrived.sum(axis=0)
-
-
-def from_everyone(shard, axis):
-    copies = jnp.broadcast_to(shard, (lax.axis_size(axis), *shard.shape))
-    return lax.all_to_all(copies, axis, split_axis=0, concat_axis=0, tiled=True)
-
-
-def over_copies(shard, axis):
-    everything = from_everyone(shard, axis)
-    return jnp.sum(everything, axis=0)
-
-
-def packed_total(arrays, axis):
-    ends = [0]
-    for a in arrays:
-        ends.append(ends[-1] + a.size)
-    subtotal = over_copies(jnp.concatenate([a.ravel() for a in arrays]), axis)
-    return tuple((subtotal[b:e].reshape(a.shape) for a, b, e in zip(arrays, ends, ends[1:])))
-
-
-def entropy_term(value):
-    return value * jnp.log(jnp.maximum(value, 1.0))
-
-
 def exchange_kernel(row_n, col_n, evm, table, out, lab, hi, s0, s1, s2, s3, g, send, recv, acc, sem, ssem, rsem):
     devices = row_n * col_n
     me = lax.axis_index("row") * col_n + lax.axis_index("col")
@@ -230,6 +196,15 @@
     )(edge_tiles, labels.reshape(-1, LANES))
 
 
+def entropy_term(value):
+    return value * jnp.log(jnp.maximum(value, 1.0))
+
+
+def row_code(r, valid, otherwise):
+    code = jnp.where(valid, (128 + (r & 127)) << ((r >> 7) & 7), otherwise)
+    return code.astype(F32).astype(BF)
+
+
 def one_hot(v, n):
     wide = v.shape[1]
     ids = lax.broadcasted_iota(I32, (256, wide), 0).astype(F32).astype(BF)
@@ -243,104 +218,218 @@
 
 
 STEP = 16
-
-
-def add_kernel(entries, counts, out):
-    out[...] = counts[...]
-
-    def body(i, _):
-        r = jnp.concatenate([entries[0, pl.ds(i * STEP + q, 1), :] for q in range(STEP)], 1)
-        c = jnp.concatenate([entries[1, pl.ds(i * STEP + q, 1), :] for q in range(STEP)], 1)
-        out[...] += lax.dot_general(
-            one_hot(r, out.shape[0]),
-            one_hot(c, out.shape[1]),
-            (((1,), (1,)), ((), ())),
-            preferred_element_type=F32,
+NT = (((1,), (1,)), ((), ()))
+
+
+def merge_kernel(
+    row_n, col_n, early, psm, pvm, flags, entries, counts,
+    updated, cost_out, accepted_out,
+    columns, picked, col_hot, arrived, packed, finals, ssem, rsem, fssem, frsem,
+):
+    i = lax.axis_index("row")
+    j = lax.axis_index("col")
+    rows_tile, cols_tile = counts.shape
+    props = psm.shape[1]
+    per_row = props // row_n
+    steps = entries.shape[1] // STEP
+    wide = STEP * LANES
+    barrier = pltpu.get_barrier_semaphore()
+    home = j // 2
+
+    for k in range(1, row_n):
+        pl.semaphore_signal(barrier, inc=1, device_id=(lax.rem(i + k, row_n), j), device_id_type=MESH)
+
+    for k in range(col_n):
+
+        @pl.when(jnp.logical_or(home != i, j != k))
+        def _():
+            pl.semaphore_signal(barrier, inc=1, device_id=(home, k), device_id_type=MESH)
+
+    for side in (0, 1):
+        for h in range(props // LANES):
+            line = pvm[side : side + 1, h * LANES : (h + 1) * LANES]
+            columns[side, h * LANES : (h + 1) * LANES, :] = jnp.broadcast_to(line, (LANES, LANES)).T
+    mine = pl.ds(pl.multiple_of(i * per_row, 8), per_row)
+    source = columns[0, mine, :]
+    target = columns[1, mine, :]
+
+    def pick(p, _):
+        s = psm[1, p] - i * rows_tile
+        inside = jnp.logical_and(s >= 0, s < rows_tile)
+        line = counts[pl.ds(jnp.clip(s, 0, rows_tile - 1), 1), :]
+        picked[pl.ds(p, 1), :] = jnp.where(inside, line, 0.0)
+        return 0
+
+    lax.fori_loop(0, props, pick, 0, unroll=8)
+
+    def pick_own(q, _):
+        s = psm[0, i * per_row + q] - i * rows_tile
+        picked[pl.ds(props + q, 1), :] = counts[pl.ds(jnp.clip(s, 0, rows_tile - 1), 1), :]
+        return 0
+
+    lax.fori_loop(0, per_row, pick_own, 0, unroll=8)
+
+    wanted = jnp.concatenate([columns[1], source], 0) - i * rows_tile
+    wanted = row_code(wanted, jnp.logical_and(wanted >= 0, wanted < rows_tile), -1)
+
+    def lanes_of(which, s):
+        return jnp.concatenate([entries[which, pl.ds(s * STEP + q, 1), :] for q in range(STEP)], 1)
+
+    def small(s, _):
+        hot = one_hot(lanes_of(1, s), cols_tile)
+        col_hot[s] = hot
+        code = row_code(lanes_of(0, s), lanes_of(0, s) >= 0, 0)
+        tall = jnp.concatenate([wanted] * STEP, 1)
+        match = jnp.where(
+            tall == jnp.broadcast_to(code, tall.shape), jnp.ones(tall.shape, BF), jnp.zeros(tall.shape, BF)
+        ).astype(F8)
+        picked[...] += lax.dot_general(match, hot, NT, preferred_element_type=F32)
+        return 0
+
+    lax.fori_loop(0, steps, small, 0)
+
+    @pl.when(home != i)
+    def _():
+        pl.semaphore_wait(barrier, row_n - 1 + col_n)
+
+    @pl.when(home == i)
+    def _():
+        pl.semaphore_wait(barrier, row_n - 1 + col_n - 1)
+
+    for k in range(1, row_n):
+        d = lax.rem(i + k, row_n)
+        pltpu.make_async_remote_copy(
+            src_ref=picked.at[pl.ds(pl.multiple_of(d * per_row, 8), per_row), :],
+            dst_ref=arrived.at[i],
+            send_sem=ssem,
+            recv_sem=rsem,
+            device_id=(d, j),
+            device_id_type=MESH,
+        ).start()
+
+    def add(s, _):
+        updated[...] += lax.dot_general(
+            one_hot(lanes_of(0, s), rows_tile), col_hot[s], NT, preferred_element_type=F32
         )
         return 0
 
-    lax.fori_loop(0, entries.shape[1] // STEP, body, 0)
-
-
-def add_entries(entries, counts):
-    return pl.pallas_call(
-        add_kernel,
-        out_shape=jax.ShapeDtypeStruct(counts.shape, F32),
-        in_specs=[pl.BlockSpec(memory_space=pltpu.VMEM)] * 2,
-        out_specs=pl.BlockSpec(memory_space=pltpu.VMEM),
-        compiler_params=pltpu.CompilerParams(vmem_limit_bytes=60 << 20),
-    )(entries, counts)
-
-
-def per_device(counts, labels, edge_tiles, proposals, accept_flags):
-    rows_tile = counts.shape[0]
-    cols_tile = counts.shape[1]
-    row_devices = lax.axis_size("row")
-    col_devices = lax.axis_size("col")
-    row_ids = jnp.arange(rows_tile, dtype=jnp.int32)
-    col_ids = jnp.arange(cols_tile, dtype=jnp.int32)
-    entries = exchange(edge_tiles, labels, row_devices, col_devices)
-    updated = add_entries(entries, counts)
-    col_index = lax.axis_index("col")
-    row_index = lax.axis_index("row")
-    mine = lax.dynamic_slice_in_dim(proposals, col_index * PROP_COL, PROP_COL, 1)
-    source = mine[0]
-    target = mine[1]
-    own_selector = (source[:, None] == col_index * cols_tile + col_ids[None, :]).astype(jnp.float32)
-    own_column = lax.dot_general(
-        own_selector,
-        updated,
-        (((1,), (1,)), ((), ())),
-        precision=lax.Precision.HIGHEST,
-        preferred_element_type=jnp.float32,
+    updated[...] = counts[...]
+    lax.fori_loop(0, early, add, 0)
+
+    most = pl.ds(0, row_n - 1)
+    pltpu.make_async_copy(arrived.at[most], arrived.at[most], rsem).wait()
+    pltpu.make_async_copy(arrived.at[most], arrived.at[most], ssem).wait()
+    arrived[i] = picked[mine, :]
+    other = jnp.sum(arrived[...], axis=0)
+    own = picked[props:, :]
+    where_at = lax.broadcasted_iota(I32, own.shape, 1) + j * cols_tile
+    wide4 = cols_tile // LANES
+    at_source = where_at == jnp.concatenate([source] * wide4, 1)
+    at_target = where_at == jnp.concatenate([target] * wide4, 1)
+    mixed = entropy_term(own + other) - entropy_term(own) - entropy_term(other)
+    parts = (
+        jnp.where(jnp.logical_or(at_source, at_target), 0.0, mixed),
+        jnp.where(at_source, own, 0.0),
+        jnp.where(at_source, other, 0.0),
+        jnp.where(at_target, other, 0.0),
+        own,
+        other,
     )
-    all_targets = proposals[1]
-    selector = (all_targets[:, None] == col_index * cols_tile + col_ids[None, :]).astype(
-        jnp.float32
-    )
-    other_column = summed_on_arrival(
-        lax.dot_general(
-            selector,
-            updated,
-            (((1,), (1,)), ((), ())),
-            precision=lax.Precision.HIGHEST,
-            preferred_element_type=jnp.float32,
-        ),
-        "col",
-        0,
-    )
-    row_global = row_index * rows_tile + row_ids
-    at_source = row_global[None, :] == source[:, None]
-    at_target = row_global[None, :] == target[:, None]
-    mixed = (
-        entropy_term(own_column + other_column)
-        - entropy_term(own_column)
-        - entropy_term(other_column)
-    )
-    pair_part = jnp.sum(jnp.where(at_source | at_target, jnp.float32(0.0), mixed), axis=1)
-    source_part = jnp.sum(jnp.where(at_source, own_column, jnp.float32(0.0)), axis=1)
-    cross_part = jnp.sum(jnp.where(at_source, other_column, jnp.float32(0.0)), axis=1)
-    target_part = jnp.sum(jnp.where(at_target, other_column, jnp.float32(0.0)), axis=1)
-    degree_part = jnp.sum(own_column, axis=1)
-    other_degree = jnp.sum(other_column, axis=1)
-    pair_sum, self_source, cross_count, self_target, degree_source, degree_target = packed_total(
-        (pair_part, source_part, cross_part, target_part, degree_part, other_degree), "row"
-    )
+    lane = lax.broadcasted_iota(I32, (per_row, LANES), 1)
+    table = jnp.zeros((per_row, LANES), F32)
+    for k, part in enumerate(parts):
+        table = jnp.where(lane == k, jnp.sum(part, axis=1, keepdims=True), table)
+    table = jnp.concatenate([table, jnp.zeros((LANES - per_row, LANES), F32)], 0).T
+    packed[...] = table[:8]
+
+    for k in range(2 * row_n):
+        d = (k // 2, 2 * i + k % 2)
+        same = jnp.logical_and(d[0] == i, d[1] == j)
+
+        @pl.when(jnp.logical_not(same))
+        def _():
+            pltpu.make_async_remote_copy(
+                src_ref=packed, dst_ref=finals.at[j], send_sem=fssem, recv_sem=frsem,
+                device_id=d, device_id_type=MESH,
+            ).start()
+
+    @pl.when(home == i)
+    def _():
+        finals[j] = packed[...]
+
+    lax.fori_loop(early, steps, add, 0)
+
+    @pl.when(home == i)
+    def _():
+        fewer = pl.ds(0, col_n - 1)
+        pltpu.make_async_copy(finals.at[fewer], finals.at[fewer], fssem).wait()
+        pltpu.make_async_copy(finals.at[fewer], finals.at[fewer], frsem).wait()
+
+    @pl.when(home != i)
+    def _():
+        pltpu.make_async_copy(finals, finals, fssem).wait()
+        pltpu.make_async_copy(finals, finals, frsem).wait()
+
+    sums = jnp.sum(finals[...], axis=0)
+    pair, self_source, cross, self_target, degree_source, degree_target = [
+        sums[k : k + 1] for k in range(6)
+    ]
     corner = (
-        entropy_term(self_source + 2.0 * cross_count + self_target)
+        entropy_term(self_source + 2.0 * cross + self_target)
         - entropy_term(self_source)
         - entropy_term(self_target)
-        - 2.0 * entropy_term(cross_count)
+        - 2.0 * entropy_term(cross)
     )
     change = (
-        -(pair_sum + 0.5 * corner)
+        -(pair + 0.5 * corner)
         + entropy_term(degree_source + degree_target)
         - entropy_term(degree_source)
         - entropy_term(degree_target)
     )
-    merge_cost = change / BLOCKS
-    accepted_cost = jnp.where(accept_flags == 1, merge_cost, jnp.float32(0.0))
-    return (updated, merge_cost, accepted_cost)
+    cost = change / BLOCKS
+    per_col = props // col_n
+    cost = jnp.where(lax.rem(j, 2) == 0, cost[:, :per_col], cost[:, per_col : 2 * per_col])
+    cost_out[...] = cost
+    accepted_out[...] = jnp.where(flags[...] == 1, cost, 0.0)
+
+
+def merge(proposals, flags, entries, counts, row_n, col_n):
+    props = proposals.shape[1]
+    per_row = props // row_n
+    rows_tile, cols_tile = counts.shape
+    vm = pl.BlockSpec(memory_space=pltpu.VMEM)
+    out16 = jax.ShapeDtypeStruct(flags.shape, F32)
+    return pl.pallas_call(
+        functools.partial(merge_kernel, row_n, col_n, 6),
+        out_shape=(jax.ShapeDtypeStruct(counts.shape, F32), out16, out16),
+        in_specs=[pl.BlockSpec(memory_space=pltpu.SMEM), vm, vm, vm, vm],
+        out_specs=(vm, vm, vm),
+        scratch_shapes=[
+            pltpu.VMEM((2, props, LANES), I32),
+            pltpu.VMEM((props + per_row, cols_tile), F32),
+            pltpu.VMEM((entries.shape[1] // STEP, cols_tile, STEP * LANES), F8),
+            pltpu.VMEM((row_n, per_row, cols_tile), F32),
+            pltpu.VMEM((8, LANES), F32),
+            pltpu.VMEM((col_n, 8, LANES), F32),
+            pltpu.SemaphoreType.DMA,
+            pltpu.SemaphoreType.DMA,
+            pltpu.SemaphoreType.DMA,
+            pltpu.SemaphoreType.DMA,
+        ],
+        compiler_params=pltpu.CompilerParams(
+            collective_id=1, has_side_effects=True, vmem_limit_bytes=60 << 20
+        ),
+    )(proposals, proposals, flags, entries, counts)
+
+
+def per_device(counts, labels, edge_tiles, proposals, accept_flags):
+    row_n = lax.axis_size("row")
+    col_n = lax.axis_size("col")
+    entries = exchange(edge_tiles, labels, row_n, col_n)
+    updated, cost, accepted = merge(
+        proposals, accept_flags.reshape(1, -1), entries, counts, row_n, col_n
+    )
+    return updated, cost.reshape(-1), accepted.reshape(-1)
 
 
 def solution(mesh):

time: 83.6 us -> 59.1 us (0.71)
  waiting for transfers between devices: 16.4 us -> 0 us
  blocking collectives: 9.38 us -> 0 us
  Pallas kernels: 46.2 us -> 54.2 us
  matrix products: 5.07 us -> 0 us
  starting transfers between devices: 3.78 us -> 0 us
  local copies, waits for them, and re-layouts: 0.87 us -> 4.11 us
  other arithmetic: 0.88 us -> 0 us
    all_to_all x1 -> x0, waiting for transfers between devices: 16.4 us -> none  [summed_on_arrival(): lax.all_to_all(blocks, axis, split_axis=0, concat_axis=0, tiled=True)]
    all_to_all x1 -> x0, blocking collectives: 9.38 us -> none  [from_everyone(): return lax.all_to_all(copies, axis, split_axis=0, concat_axis=0, tiled=True)]
    pallas_call x1, Pallas kernels: 14.2 us -> 22.1 us  [merge(): pl.pallas_call(functools.partial(merge_kernel, row_n, col_n, 6), out_shap...]
    dot_general x2 -> x0, matrix products: 5.07 us -> none  [the longest x1 3.84 us: per_device(): lax.dot_general(selector, updated, (((1,), (1,)), ((), ())), precision=la...]
    unnamed x6 -> x7, local copies, waits for them, and re-layouts: 0.01 us -> 4.11 us
    all_to_all x1 -> x0, starting transfers between devices: 3.78 us -> none  [summed_on_arrival(): lax.all_to_all(blocks, axis, split_axis=0, concat_axis=0, tiled=True)]
  transfers between devices with their start and end apart: 1 -> 0, of which waited for: 1 -> 0; matrix products, arithmetic and copies ran while one was open for 0% -> 0% of each run, Pallas kernels for 0% -> 0%
where the time goes in v2:
time: 59.1 us; the launch traced here: 58.9 us
  Pallas kernels  54.2 us (92%)
  local copies, waits for them, and re-layouts  4.11 us (7%)
  between operations  0.66 us (1%)
    pallas_call x1, Pallas kernels, exchange(): pl.pallas_call(functools.partial(exchange_kernel, row_n, col_n), out_shap...  32.1 us
    pallas_call x1, Pallas kernels, merge(): pl.pallas_call(functools.partial(merge_kernel, row_n, col_n, 6), out_shap...  22.1 us
    unnamed x7, local copies, waits for them, and re-layouts  4.11 us

profile of v2, /device:TPU:1, one launch (start us, length us, event | category | flops | bytes accessed | tf_op | source)
XLA Modules:
  0.0 58.9 jit_solution(17869662917531942947)
XLA Ops:
  0.6 32.1 %shard_map.76.entries = s32[2,144,128]{2,1,0:T(8,128)} custom-call(s32[32,2,128]{2,1,0:T(2,128)} %evm.1, s32[7680,128]{1,0:T(8,128)} %bitcast.4), custom_call_target="tpu_custom_call" | custom-call | tf_op jit(solution)/shard_map/pallas_call | solution.py:175
  32.7 22.1 %shard_map.77 = (f32[1024,512]{1,0:T(8,128)}, f32[1,16]{1,0:T(1,128)}, f32[1,16]{1,0:T(1,128)}) custom-call(s32[2,256]{1,0:T(2,128)} %pvm.1, s32[2,256]{1,0:T(2,128)} %pvm.1, s32[1,16]{1,0:T(1,128)} %bitcast.5, s32[2,144,128]{2,1,0:T(8,128)} %shard_map.76.entries, f32[1024,512]{1,0:T(8,128)} %counts.1), custom_call_target="tpu_custom_call" | custom-call | tf_op jit(solution)/shard_map/pallas_call | solution.py:402
  54.8 0.0 copy-start.1
  54.8 0.0 copy-start
  54.8 3.1 %copy.11 = f32[1024,512]{1,0:T(8,128)} copy(f32[1024,512]{1,0:T(8,128)} %get-tuple-element.12) | data formatting | bytes 4194304
  57.9 0.0 copy-done.1
  57.9 0.5 copy.12
  58.4 0.0 copy-done
  58.4 0.5 copy.13
Async XLA Ops:
  54.8 3.1 %copy-start.1 = (f32[1,16]{1,0:T(1,128)S(1)}, f32[1,16]{1,0:T(1,128)}, u32[]{:S(2)}) copy-start(f32[1,16]{1,0:T(1,128)} %get-tuple-element.7) | copy-start | bytes 196
  54.8 3.6 %copy-start = (f32[1,16]{1,0:T(1,128)S(1)}, f32[1,16]{1,0:T(1,128)}, u32[]{:S(2)}) copy-start(f32[1,16]{1,0:T(1,128)} %get-tuple-element.8) | copy-start | bytes 196

commit v3 on v2

v3 whole, which is shorter than its diff:
```python
import functools

import jax
import jax.numpy as jnp
from jax import lax
from jax.experimental import pallas as pl
from jax.experimental.pallas import tpu as pltpu
from jax.sharding import PartitionSpec as P

I32 = jnp.int32
F32 = jnp.float32
BF = jnp.bfloat16
F8 = jnp.float8_e4m3fn
LANES = 128
BLOCKS = 8192
MESH = pl.DeviceIdType.MESH


def start_gather(evm, hi, sms, sem):
    hi[...] = lax.shift_right_logical(evm[...], 7)
    for k in range(len(sms)):
        pltpu.make_async_copy(hi.at[k], sms[k], sem.at[k]).start()


def gather_labels(evm, table, lab, hi, sms, g, sem):
    tiles = evm.shape[0]
    depth = len(sms)
    sub = lax.broadcasted_iota(I32, (LANES, LANES), 0)

    def finish(t, slot):
        for side in (0, 1):
            lanes = evm[t, pl.ds(side, 1), :] & (LANES - 1)
            picked = jnp.where(sub == lanes, g[slot, side].T, 0)
            lab[pl.ds(side, 1), pl.ds(pl.multiple_of(t * LANES, LANES), LANES)] = jnp.sum(
                picked, axis=0, keepdims=True
            )

    def body(u, _):
        for k in range(depth):
            t = depth * u + k
            pltpu.make_async_copy(hi.at[t], sms[k], sem.at[k]).wait()
            finish(jnp.maximum(t - 1, 0), (k + 1) % 2)
            for side in (0, 1):
                for e in range(LANES):
                    g[k % 2, side, pl.ds(e, 1), :] = table[pl.ds(sms[k][side, e], 1), :]
            later = jnp.minimum(t + depth, tiles - 1)
            pltpu.make_async_copy(hi.at[later], sms[k], sem.at[k]).start()
        return 0

    lax.fori_loop(0, tiles // depth, body, 0)
    for k in range(depth):
        pltpu.make_async_copy(hi.at[tiles - 1], sms[k], sem.at[k]).wait()
    finish(tiles - 1, (depth - 1) % 2)


BLOCK = 256
GROUP = 8
NT = (((1,), (1,)), ((), ()))


def place_entries(lab, send, acc, rows_tile, cols_tile, col_devices):
    edges = lab.shape[1]
    wide = GROUP * BLOCK
    upper = (
        lax.broadcasted_iota(I32, (BLOCK, BLOCK), 0) <= lax.broadcasted_iota(I32, (BLOCK, BLOCK), 1)
    ).astype(F32).astype(BF)
    dev16 = lax.broadcasted_iota(I32, (LANES, BLOCK), 0).astype(F32).astype(BF)
    one = jnp.ones((LANES, BLOCK), BF)
    zero = jnp.zeros((LANES, BLOCK), BF)
    tail16 = (lax.broadcasted_iota(I32, (16, BLOCK), 0) + LANES).astype(F32).astype(BF)
    tail_zero = jnp.zeros((16, BLOCK), BF)
    acc[...] = jnp.zeros_like(acc)

    def cast(x):
        return x.astype(F32).astype(BF)

    def group(side):
        def body(u, base):
            lanes = pl.ds(pl.multiple_of(u * wide, wide), wide)
            rlab = lab[pl.ds(side, 1), lanes]
            clab = lab[pl.ds(1 - side, 1), lanes]
            owner16 = cast((rlab // rows_tile) * col_devices + clab // cols_tile)
            row = rlab % rows_tile + 1
            col = clab % cols_tile
            pieces = [cast(row & -32), cast(col & -32), cast(row & 31), cast(col & 31)]
            hots = []
            for q in range(GROUP):
                cut = slice(q * BLOCK, (q + 1) * BLOCK)
                hots.append(
                    jnp.where(dev16 == jnp.broadcast_to(owner16[:, cut], dev16.shape), one, zero)
                )
            within = jnp.dot(jnp.concatenate(hots, 0), upper, preferred_element_type=F32)
            total = None
            for q in range(GROUP):
                cut = slice(q * BLOCK, (q + 1) * BLOCK)
                w = within[q * LANES : (q + 1) * LANES]
                running = w + jnp.concatenate([base, base], 1)
                slot = jnp.sum(hots[q].astype(F32) * running, axis=0, keepdims=True) - 1.0
                base = base + jnp.broadcast_to(w[:, BLOCK - 1 :], base.shape)
                slot16 = slot.astype(BF)
                main = dev16 == jnp.broadcast_to(slot16, dev16.shape)
                tail = tail16 == jnp.broadcast_to(slot16, tail16.shape)
                spread = [
                    jnp.where(main, jnp.broadcast_to(v[:, cut], dev16.shape), zero) for v in pieces
                ] + [
                    jnp.where(tail, jnp.broadcast_to(v[:, cut], tail16.shape), tail_zero) for v in pieces
                ]
                part = lax.dot_general(
                    jnp.concatenate(spread, 0), hots[q], NT, preferred_element_type=F32
                )
                total = part if total is None else total + part
            acc[...] += total
            return base

        return body

    base = jnp.zeros((LANES, LANES), F32)
    for side in (0, 1):
        base = lax.fori_loop(0, edges // wide, group(side), base)
    for k in range(2):
        high = acc[k * LANES : (k + 1) * LANES]
        low = acc[(k + 2) * LANES : (k + 3) * LANES]
        send[k] = (high + low).T.astype(I32)
    tail = acc[4 * LANES : 4 * LANES + 32] + acc[4 * LANES + 32 :]
    send[2] = jnp.concatenate([tail, jnp.zeros((LANES - 32, LANES), F32)], 0).T.astype(I32)


def entropy_term(value):
    return value * jnp.log(jnp.maximum(value, 1.0))


def row_code(r, valid, otherwise):
    code = jnp.where(valid, (128 + (r & 127)) << ((r >> 7) & 7), otherwise)
    return code.astype(F32).astype(BF)


def one_hot(v, n):
    wide = v.shape[1]
    ids = lax.broadcasted_iota(I32, (256, wide), 0).astype(F32).astype(BF)
    one = jnp.ones((256, wide), BF)
    zero = jnp.zeros((256, wide), BF)
    out = []
    for b in range(n // 256):
        w = jnp.where((v >> 8) == b, v & 255, -1).astype(F32).astype(BF)
        out.append(jnp.where(ids == jnp.broadcast_to(w, ids.shape), one, zero).astype(F8))
    return jnp.concatenate(out, 0)


STEP = 16


def ingest_kernel(
    row_n, col_n, early, proposals_in, edges_in, flags_in, table_in, counts_in,
    updated, cost_out, accepted_out,
    table, counts, evm, psm, pvm, flags, lab, hi, s0, s1, s2, s3, g, send, recv, tails, acc,
    columns, picked, col_hot, arrived, packed, finals,
    hsem, lsem, ssem, rsem, essem, ersem, fssem, frsem,
):
    devices = row_n * col_n
    i = lax.axis_index("row")
    j = lax.axis_index("col")
    me = i * col_n + j
    rows_tile, cols_tile = counts.shape
    props = psm.shape[1]
    per_row = props // row_n
    home = j // 2
    sms = (s0, s1, s2, s3)
    barrier = pltpu.get_barrier_semaphore()

    load_table = pltpu.make_async_copy(table_in, table, lsem.at[0])
    load_counts = pltpu.make_async_copy(counts_in, counts, lsem.at[1])
    load_edges = pltpu.make_async_copy(edges_in, evm, lsem.at[2])
    others = (
        pltpu.make_async_copy(proposals_in, pvm, lsem.at[3]),
        pltpu.make_async_copy(proposals_in, psm, lsem.at[4]),
        pltpu.make_async_copy(flags_in, flags, lsem.at[5]),
    )
    load_edges.start()
    load_table.start()
    for load in others:
        load.start()
    load_counts.start()

    def greet(k, _):
        d = lax.rem(me + k, devices)
        pl.semaphore_signal(barrier, inc=1, device_id=(d // col_n, lax.rem(d, col_n)), device_id_type=MESH)
        return 0

    lax.fori_loop(1, devices, greet, 0)
    load_edges.wait()
    start_gather(evm, hi, sms, hsem)
    for load in others:
        load.wait()
    for side in (0, 1):
        for h in range(props // LANES):
            line = pvm[side : side + 1, h * LANES : (h + 1) * LANES]
            columns[side, h * LANES : (h + 1) * LANES, :] = jnp.broadcast_to(line, (LANES, LANES)).T
    load_table.wait()
    gather_labels(evm, table, lab, hi, sms, g, hsem)
    place_entries(lab, send, acc, rows_tile, cols_tile, col_n)
    pl.semaphore_wait(barrier, devices - 1)

    def push(k, _):
        d = lax.rem(me + k, devices)
        pltpu.make_async_remote_copy(
            src_ref=send.at[:, pl.ds(d, 1), :],
            dst_ref=recv.at[:, pl.ds(me, 1), :],
            send_sem=ssem,
            recv_sem=rsem.at[i],
            device_id=(d // col_n, lax.rem(d, col_n)),
            device_id_type=MESH,
        ).start()
        return 0

    lax.fori_loop(1, devices, push, 0)
    recv[:, pl.ds(me, 1), :] = send[:, pl.ds(me, 1), :]
    load_counts.wait()

    def pick(p, _):
        s = psm[1, p] - i * rows_tile
        inside = jnp.logical_and(s >= 0, s < rows_tile)
        line = counts[pl.ds(jnp.clip(s, 0, rows_tile - 1), 1), :]
        picked[pl.ds(p, 1), :] = jnp.where(inside, line, 0.0)
        return 0

    lax.fori_loop(0, props, pick, 0, unroll=8)

    def pick_own(q, _):
        s = psm[0, i * per_row + q] - i * rows_tile
        picked[pl.ds(props + q, 1), :] = counts[pl.ds(jnp.clip(s, 0, rows_tile - 1), 1), :]
        return 0

    lax.fori_loop(0, per_row, pick_own, 0, unroll=8)
    updated[...] = counts[...]

    mine = pl.ds(pl.multiple_of(i * per_row, 8), per_row)
    source = columns[0, mine, :]
    target = columns[1, mine, :]
    wanted = jnp.concatenate([columns[1], source], 0) - i * rows_tile
    wanted = row_code(wanted, jnp.logical_and(wanted >= 0, wanted < rows_tile), -1)

    def lanes_of(ref, s):
        return jnp.concatenate([ref[pl.ds(s * STEP + q, 1), :] for q in range(STEP)], 1)

    def small(s, rows, cols):
        hot = one_hot(cols, cols_tile)
        col_hot[s] = hot
        code = row_code(rows, rows >= 0, 0)
        tall = jnp.concatenate([wanted] * STEP, 1)
        match = jnp.where(
            tall == jnp.broadcast_to(code, tall.shape), jnp.ones(tall.shape, BF), jnp.zeros(tall.shape, BF)
        ).astype(F8)
        picked[...] += lax.dot_general(match, hot, NT, preferred_element_type=F32)

    part = recv.at[:, pl.ds(0, col_n - 1), :]
    pltpu.make_async_copy(part, part, rsem.at[i]).wait()
    small(i, lanes_of(recv.at[0], i) - 1, lanes_of(recv.at[1], i))

    def arrive(k, _):
        s = lax.rem(i - k + row_n, row_n)
        part = recv.at[:, pl.ds(0, col_n), :]
        pltpu.make_async_copy(part, part, rsem.at[s]).wait()
        small(s, lanes_of(recv.at[0], s) - 1, lanes_of(recv.at[1], s))
        return 0

    lax.fori_loop(1, row_n, arrive, 0)
    tails[...] = recv[2].T
    last_rows = jnp.concatenate([tails[q : q + 1] for q in range(16)], 1) - 1
    last_cols = jnp.concatenate([tails[q : q + 1] for q in range(16, 32)], 1)
    small(row_n, last_rows, last_cols)

    for k in range(1, row_n):
        d = lax.rem(i + k, row_n)
        pltpu.make_async_remote_copy(
            src_ref=picked.at[pl.ds(pl.multiple_of(d * per_row, 8), per_row), :],
            dst_ref=arrived.at[i],
            send_sem=essem,
            recv_sem=ersem,
            device_id=(d, j),
            device_id_type=MESH,
        ).start()

    def add(s, rows):
        updated[...] += lax.dot_general(
            one_hot(rows, rows_tile), col_hot[s], NT, preferred_element_type=F32
        )

    def add_step(s, _):
        add(s, lanes_of(recv.at[0], s) - 1)
        return 0

    lax.fori_loop(0, early, add_step, 0)
    rest = pl.ds(0, devices - 1)
    pltpu.make_async_copy(send.at[:, rest, :], send.at[:, rest, :], ssem).wait()

    most = pl.ds(0, row_n - 1)
    pltpu.make_async_copy(arrived.at[most], arrived.at[most], ersem).wait()
    pltpu.make_async_copy(arrived.at[most], arrived.at[most], essem).wait()
    arrived[i] = picked[mine, :]
    other = jnp.sum(arrived[...], axis=0)
    own = picked[props:, :]
    where_at = lax.broadcasted_iota(I32, own.shape, 1) + j * cols_tile
    wide4 = cols_tile // LANES
    at_source = where_at == jnp.concatenate([source] * wide4, 1)
    at_target = where_at == jnp.concatenate([target] * wide4, 1)
    mixed = entropy_term(own + other) - entropy_term(own) - entropy_term(other)
    parts = (
        jnp.where(jnp.logical_or(at_source, at_target), 0.0, mixed),
        jnp.where(at_source, own, 0.0),
        jnp.where(at_source, other, 0.0),
        jnp.where(at_target, other, 0.0),
        own,
        other,
    )
    lane = lax.broadcasted_iota(I32, (per_row, LANES), 1)
    table = jnp.zeros((per_row, LANES), F32)
    for k, part in enumerate(parts):
        table = jnp.where(lane == k, jnp.sum(part, axis=1, keepdims=True), table)
    table = jnp.concatenate([table, jnp.zeros((LANES - per_row, LANES), F32)], 0).T
    packed[...] = table[:8]

    for k in range(2 * row_n):
        d = (k // 2, 2 * i + k % 2)
        same = jnp.logical_and(d[0] == i, d[1] == j)

        @pl.when(jnp.logical_not(same))
        def _():
            pltpu.make_async_remote_copy(
                src_ref=packed, dst_ref=finals.at[j], send_sem=fssem, recv_sem=frsem,
                device_id=d, device_id_type=MESH,
            ).start()

    @pl.when(home == i)
    def _():
        finals[j] = packed[...]

    lax.fori_loop(early, row_n, add_step, 0)
    add(row_n, jnp.concatenate([tails[q : q + 1] for q in range(16)], 1) - 1)

    @pl.when(home == i)
    def _():
        fewer = pl.ds(0, col_n - 1)
        pltpu.make_async_copy(finals.at[fewer], finals.at[fewer], fssem).wait()
        pltpu.make_async_copy(finals.at[fewer], finals.at[fewer], frsem).wait()

    @pl.when(home != i)
    def _():
        pltpu.make_async_copy(finals, finals, fssem).wait()
        pltpu.make_async_copy(finals, finals, frsem).wait()

    sums = jnp.sum(finals[...], axis=0)
    pair, self_source, cross, self_target, degree_source, degree_target = [
        sums[k : k + 1] for k in range(6)
    ]
    corner = (
        entropy_term(self_source + 2.0 * cross + self_target)
        - entropy_term(self_source)
        - entropy_term(self_target)
        - 2.0 * entropy_term(cross)
    )
    change = (
        -(pair + 0.5 * corner)
        + entropy_term(degree_source + degree_target)
        - entropy_term(degree_source)
        - entropy_term(degree_target)
    )
    cost = change / BLOCKS
    per_col = props // col_n
    cost = jnp.where(lax.rem(j, 2) == 0, cost[:, :per_col], cost[:, per_col : 2 * per_col])
    cost_out[...] = cost
    accepted_out[...] = jnp.where(flags[...] == 1, cost, 0.0)


def ingest(proposals, edge_tiles, flags, labels, counts, row_n, col_n):
    props = proposals.shape[1]
    per_row = props // row_n
    rows_tile, cols_tile = counts.shape
    tiles = edge_tiles.shape[0]
    devices = row_n * col_n
    table = labels.reshape(-1, LANES)
    vm = pl.BlockSpec(memory_space=pltpu.VMEM)
    anywhere = pl.BlockSpec(memory_space=pltpu.HBM)
    small = pltpu.SMEM((2, LANES), I32)
    dma = pltpu.SemaphoreType.DMA
    out16 = pltpu.VMEM(flags.shape, F32)
    return pl.pallas_call(
        functools.partial(ingest_kernel, row_n, col_n, 6),
        out_shape=(pltpu.VMEM(counts.shape, F32), out16, out16),
        in_specs=[anywhere] * 5,
        out_specs=(vm, vm, vm),
        scratch_shapes=[
            pltpu.VMEM(table.shape, I32),
            pltpu.VMEM(counts.shape, F32),
            pltpu.VMEM(edge_tiles.shape, I32),
            pltpu.SMEM(proposals.shape, I32),
            pltpu.VMEM(proposals.shape, I32),
            pltpu.VMEM(flags.shape, I32),
            pltpu.VMEM((2, tiles * LANES), I32),
            pltpu.VMEM(edge_tiles.shape, I32),
            small,
            small,
            small,
            small,
            pltpu.VMEM((2, 2, LANES, LANES), I32),
            pltpu.VMEM((3, devices, LANES), I32),
            pltpu.VMEM((3, devices, LANES), I32),
            pltpu.VMEM((LANES, LANES), I32),
            pltpu.VMEM((576, LANES), F32),
            pltpu.VMEM((2, props, LANES), I32),
            pltpu.VMEM((props + per_row, cols_tile), F32),
            pltpu.VMEM((row_n + 1, cols_tile, STEP * LANES), F8),
            pltpu.VMEM((row_n, per_row, cols_tile), F32),
            pltpu.VMEM((8, LANES), F32),
            pltpu.VMEM((col_n, 8, LANES), F32),
            dma((4,)),
            dma((6,)),
            dma,
            dma((row_n,)),
            dma,
            dma,
            dma,
            dma,
        ],
        compiler_params=pltpu.CompilerParams(
            collective_id=0, has_side_effects=True, vmem_limit_bytes=32 << 20
        ),
    )(*[
        pltpu.with_memory_space_constraint(x, pltpu.HBM)
        for x in (proposals, edge_tiles, flags, table, counts)
    ])


def per_device(counts, labels, edge_tiles, proposals, accept_flags):
    row_n = lax.axis_size("row")
    col_n = lax.axis_size("col")
    updated, cost, accepted = ingest(
        proposals, edge_tiles, accept_flags.reshape(1, -1), labels, counts, row_n, col_n
    )
    return updated, cost.reshape(-1), accepted.reshape(-1)


def solution(mesh):
    return jax.shard_map(
        per_device,
        mesh=mesh,
        in_specs=(P("row", "col"), P(), P(("row", "col"), None, None), P(), P("col")),
        out_specs=(P("row", "col"), P("col"), P("col")),
        check_vma=False,
    )
```

time: 59.1 us -> 46.4 us (0.79)
  Pallas kernels: 54.2 us -> 43.3 us
  local copies, waits for them, and re-layouts: 4.11 us -> 2.34 us
    pallas_call x2 -> x1, Pallas kernels: 54.2 us -> 43.3 us  [ingest(): pl.pallas_call(functools.partial(ingest_kernel, row_n, col_n, 6), out_sha...]
    unnamed x7 -> x3, local copies, waits for them, and re-layouts: 4.11 us -> 2.34 us
where the time goes in v3:
time: 46.4 us; the launch traced here: 46.3 us
  Pallas kernels  43.3 us (93%)
  local copies, waits for them, and re-layouts  2.34 us (5%)
  between operations  0.64 us (1%)
    pallas_call x1, Pallas kernels, ingest(): pl.pallas_call(functools.partial(ingest_kernel, row_n, col_n, 6), out_sha...  43.3 us
    unnamed x3, local copies, waits for them, and re-layouts  2.34 us

profile of v3, /device:TPU:1, one launch (start us, length us, event | category | flops | bytes accessed | tf_op | source)
XLA Modules:
  0.0 46.3 jit_solution(10786865709790287422)
XLA Ops:
  0.6 43.3 %shard_map.76 = (f32[1024,512]{1,0:T(8,128)S(1)}, f32[1,16]{1,0:T(1,128)S(1)}, f32[1,16]{1,0:T(1,128)S(1)}) custom-call(s32[2,256]{1,0:T(2,128)} %proposals_in.1, s32[32,2,128]{2,1,0:T(2,128)} %edges_in.1, s32[1,16]{1,0:T(1,128)} %bitcast.7, s32[7680,128]{1,0:T(8,128)} %bitcast.6, f32[1024,512]{1,0:T(8,128)} %counts_in.1), custom_call_target="tpu_custom_call" | custom-call | tf_op jit(solution)/shard_map/pallas_call | solution.py:386
  44.0 1.3 %copy.11 = f32[1024,512]{1,0:T(8,128)} copy(f32[1024,512]{1,0:T(8,128)S(1)} %get-tuple-element.9) | data formatting | bytes 4194304
  45.3 0.5 %copy.12 = f32[16]{0:T(128)} copy(f32[16]{0:T(128)S(1)} %bitcast.5) | data formatting | bytes 128
  45.8 0.5 %copy.13 = f32[16]{0:T(128)} copy(f32[16]{0:T(128)S(1)} %bitcast.4) | data formatting | bytes 128

commit v4 on v3

--- a/solution.py
+++ b/solution.py
@@ -31,9 +31,7 @@
         for side in (0, 1):
             lanes = evm[t, pl.ds(side, 1), :] & (LANES - 1)
             picked = jnp.where(sub == lanes, g[slot, side].T, 0)
-            lab[pl.ds(side, 1), pl.ds(pl.multiple_of(t * LANES, LANES), LANES)] = jnp.sum(
-                picked, axis=0, keepdims=True
-            )
+            lab[side, pl.ds(t, 1), :] = jnp.sum(picked, axis=0, keepdims=True)
 
     def body(u, _):
         for k in range(depth):
@@ -54,13 +52,23 @@
 
 
 BLOCK = 256
-GROUP = 8
+GROUP = 16
+SPREAD = 16
 NT = (((1,), (1,)), ((), ()))
 
 
-def place_entries(lab, send, acc, rows_tile, cols_tile, col_devices):
-    edges = lab.shape[1]
-    wide = GROUP * BLOCK
+def place_entries(lab, enc, hot, slots, send, acc, rows_tile, cols_tile, col_devices):
+    tiles = lab.shape[1]
+    pair = BLOCK // LANES
+    row_bits = rows_tile.bit_length() - 1
+    col_bits = cols_tile.bit_length() - 1
+    for side in (0, 1):
+        row, col = lab[side], lab[1 - side]
+        enc[side, 0] = ((row >> row_bits) * col_devices + (col >> col_bits)).astype(F32)
+        row = (row & (rows_tile - 1)) + 1
+        col = col & (cols_tile - 1)
+        for k, piece in enumerate((row & -32, col & -32, row & 31, col & 31)):
+            enc[side, k + 1] = piece.astype(F32)
     upper = (
         lax.broadcasted_iota(I32, (BLOCK, BLOCK), 0) <= lax.broadcasted_iota(I32, (BLOCK, BLOCK), 1)
     ).astype(F32).astype(BF)
@@ -71,52 +79,58 @@
     tail_zero = jnp.zeros((16, BLOCK), BF)
     acc[...] = jnp.zeros_like(acc)
 
-    def cast(x):
-        return x.astype(F32).astype(BF)
-
-    def group(side):
+    def line(ref, q):
+        return jnp.concatenate([ref[pl.ds(q * pair + n, 1), :] for n in range(pair)], 1).astype(BF)
+
+    def rank(side):
         def body(u, base):
-            lanes = pl.ds(pl.multiple_of(u * wide, wide), wide)
-            rlab = lab[pl.ds(side, 1), lanes]
-            clab = lab[pl.ds(1 - side, 1), lanes]
-            owner16 = cast((rlab // rows_tile) * col_devices + clab // cols_tile)
-            row = rlab % rows_tile + 1
-            col = clab % cols_tile
-            pieces = [cast(row & -32), cast(col & -32), cast(row & 31), cast(col & 31)]
             hots = []
             for q in range(GROUP):
-                cut = slice(q * BLOCK, (q + 1) * BLOCK)
-                hots.append(
-                    jnp.where(dev16 == jnp.broadcast_to(owner16[:, cut], dev16.shape), one, zero)
-                )
+                owner = line(enc.at[side, 0], u * GROUP + q)
+                hots.append(jnp.where(dev16 == jnp.broadcast_to(owner, dev16.shape), one, zero))
+            lanes = pl.ds(pl.multiple_of(u * GROUP * BLOCK, GROUP * BLOCK), GROUP * BLOCK)
+            hot[side, :, lanes] = jnp.concatenate(hots, 1)
             within = jnp.dot(jnp.concatenate(hots, 0), upper, preferred_element_type=F32)
-            total = None
             for q in range(GROUP):
-                cut = slice(q * BLOCK, (q + 1) * BLOCK)
                 w = within[q * LANES : (q + 1) * LANES]
                 running = w + jnp.concatenate([base, base], 1)
-                slot = jnp.sum(hots[q].astype(F32) * running, axis=0, keepdims=True) - 1.0
+                slot = jnp.sum(jnp.where(hots[q].astype(F32) > 0.0, running, 0.0), axis=0, keepdims=True) - 1.0
+                for n in range(pair):
+                    slots[side, pl.ds((u * GROUP + q) * pair + n, 1), :] = slot[:, n * LANES : (n + 1) * LANES]
                 base = base + jnp.broadcast_to(w[:, BLOCK - 1 :], base.shape)
-                slot16 = slot.astype(BF)
-                main = dev16 == jnp.broadcast_to(slot16, dev16.shape)
-                tail = tail16 == jnp.broadcast_to(slot16, tail16.shape)
-                spread = [
-                    jnp.where(main, jnp.broadcast_to(v[:, cut], dev16.shape), zero) for v in pieces
-                ] + [
-                    jnp.where(tail, jnp.broadcast_to(v[:, cut], tail16.shape), tail_zero) for v in pieces
-                ]
-                part = lax.dot_general(
-                    jnp.concatenate(spread, 0), hots[q], NT, preferred_element_type=F32
+            return base
+
+        return body
+
+    def spread(side):
+        def body(u, _):
+            columns = []
+            for q in range(SPREAD):
+                at = u * SPREAD + q
+                slot = line(slots.at[side], at)
+                main = dev16 == jnp.broadcast_to(slot, dev16.shape)
+                tail = tail16 == jnp.broadcast_to(slot, tail16.shape)
+                pieces = [line(enc.at[side, k], at) for k in range(1, 5)]
+                columns.append(
+                    jnp.concatenate(
+                        [jnp.where(main, jnp.broadcast_to(v, dev16.shape), zero) for v in pieces]
+                        + [jnp.where(tail, jnp.broadcast_to(v, tail16.shape), tail_zero) for v in pieces],
+                        0,
+                    )
                 )
-                total = part if total is None else total + part
-            acc[...] += total
-            return base
+            lanes = pl.ds(pl.multiple_of(u * SPREAD * BLOCK, SPREAD * BLOCK), SPREAD * BLOCK)
+            acc[...] += lax.dot_general(
+                jnp.concatenate(columns, 1), hot[side, :, lanes], NT, preferred_element_type=F32
+            )
+            return 0
 
         return body
 
     base = jnp.zeros((LANES, LANES), F32)
     for side in (0, 1):
-        base = lax.fori_loop(0, edges // wide, group(side), base)
+        base = lax.fori_loop(0, tiles // (GROUP * pair), rank(side), base)
+    for side in (0, 1):
+        lax.fori_loop(0, tiles // (SPREAD * pair), spread(side), 0)
     for k in range(2):
         high = acc[k * LANES : (k + 1) * LANES]
         low = acc[(k + 2) * LANES : (k + 3) * LANES]
@@ -152,7 +166,7 @@
 def ingest_kernel(
     row_n, col_n, early, proposals_in, edges_in, flags_in, table_in, counts_in,
     updated, cost_out, accepted_out,
-    table, counts, evm, psm, pvm, flags, lab, hi, s0, s1, s2, s3, g, send, recv, tails, acc,
+    table, counts, evm, psm, pvm, near, flags, lab, enc, hot, slots, hi, s0, s1, s2, s3, g, send, recv, tails, acc,
     columns, picked, col_hot, arrived, packed, finals,
     hsem, lsem, ssem, rsem, essem, ersem, fssem, frsem,
 ):
@@ -161,7 +175,7 @@
     j = lax.axis_index("col")
     me = i * col_n + j
     rows_tile, cols_tile = counts.shape
-    props = psm.shape[1]
+    props = pvm.shape[1]
     per_row = props // row_n
     home = j // 2
     sms = (s0, s1, s2, s3)
@@ -172,66 +186,76 @@
     load_edges = pltpu.make_async_copy(edges_in, evm, lsem.at[2])
     others = (
         pltpu.make_async_copy(proposals_in, pvm, lsem.at[3]),
-        pltpu.make_async_copy(proposals_in, psm, lsem.at[4]),
         pltpu.make_async_copy(flags_in, flags, lsem.at[5]),
     )
     load_edges.start()
+    load_updated = pltpu.make_async_copy(counts_in, updated, lsem.at[6])
+    load_near = pltpu.make_async_copy(near, psm, lsem.at[4])
     load_table.start()
     for load in others:
         load.start()
-    load_counts.start()
-
-    def greet(k, _):
-        d = lax.rem(me + k, devices)
-        pl.semaphore_signal(barrier, inc=1, device_id=(d // col_n, lax.rem(d, col_n)), device_id_type=MESH)
-        return 0
-
-    lax.fori_loop(1, devices, greet, 0)
+
+    def peer(r, c):
+        return lax.rem(i + r, row_n), lax.rem(j + c, col_n)
+
+    def greet(r, _, first=0):
+        for c in range(first, col_n):
+            pl.semaphore_signal(barrier, inc=1, device_id=peer(r, c), device_id_type=MESH)
+        return 0
+
+    greet(0, 0, 1)
+    lax.fori_loop(1, row_n, greet, 0)
     load_edges.wait()
     start_gather(evm, hi, sms, hsem)
     for load in others:
         load.wait()
+    near[...] = jnp.clip(pvm[...] - i * rows_tile, 0, rows_tile - 1)
+    load_near.start()
     for side in (0, 1):
         for h in range(props // LANES):
             line = pvm[side : side + 1, h * LANES : (h + 1) * LANES]
             columns[side, h * LANES : (h + 1) * LANES, :] = jnp.broadcast_to(line, (LANES, LANES)).T
+    load_near.wait()
     load_table.wait()
+    load_counts.start()
+    load_updated.start()
     gather_labels(evm, table, lab, hi, sms, g, hsem)
-    place_entries(lab, send, acc, rows_tile, cols_tile, col_n)
+    place_entries(lab, enc, hot, slots, send, acc, rows_tile, cols_tile, col_n)
     pl.semaphore_wait(barrier, devices - 1)
 
-    def push(k, _):
-        d = lax.rem(me + k, devices)
-        pltpu.make_async_remote_copy(
-            src_ref=send.at[:, pl.ds(d, 1), :],
-            dst_ref=recv.at[:, pl.ds(me, 1), :],
-            send_sem=ssem,
-            recv_sem=rsem.at[i],
-            device_id=(d // col_n, lax.rem(d, col_n)),
-            device_id_type=MESH,
-        ).start()
-        return 0
-
-    lax.fori_loop(1, devices, push, 0)
+    def push(r, _, first=0):
+        for c in range(first, col_n):
+            d = peer(r, c)
+            at = pl.ds(d[0] * col_n + d[1], 1)
+            pltpu.make_async_remote_copy(
+                src_ref=send.at[:, at, :],
+                dst_ref=recv.at[:, pl.ds(me, 1), :],
+                send_sem=ssem,
+                recv_sem=rsem.at[i],
+                device_id=d,
+                device_id_type=MESH,
+            ).start()
+        return 0
+
+    push(0, 0, 1)
+    lax.fori_loop(1, row_n, push, 0)
     recv[:, pl.ds(me, 1), :] = send[:, pl.ds(me, 1), :]
     load_counts.wait()
 
-    def pick(p, _):
-        s = psm[1, p] - i * rows_tile
-        inside = jnp.logical_and(s >= 0, s < rows_tile)
-        line = counts[pl.ds(jnp.clip(s, 0, rows_tile - 1), 1), :]
-        picked[pl.ds(p, 1), :] = jnp.where(inside, line, 0.0)
-        return 0
-
-    lax.fori_loop(0, props, pick, 0, unroll=8)
-
-    def pick_own(q, _):
-        s = psm[0, i * per_row + q] - i * rows_tile
-        picked[pl.ds(props + q, 1), :] = counts[pl.ds(jnp.clip(s, 0, rows_tile - 1), 1), :]
-        return 0
-
-    lax.fori_loop(0, per_row, pick_own, 0, unroll=8)
-    updated[...] = counts[...]
+    def pick(u, _):
+        for q in range(8):
+            p = u * 8 + q
+            picked[pl.ds(p, 1), :] = counts[pl.ds(psm[1, p], 1), :]
+        return 0
+
+    lax.fori_loop(0, props // 8, pick, 0)
+    for q in range(per_row):
+        picked[props + q : props + q + 1, :] = counts[pl.ds(psm[0, i * per_row + q], 1), :]
+    apart = columns[1] - i * rows_tile
+    inside = jnp.logical_and(apart >= 0, apart < rows_tile)
+    picked[:props, :] = jnp.where(
+        jnp.concatenate([inside] * (cols_tile // LANES), 1), picked[:props, :], 0.0
+    )
 
     mine = pl.ds(pl.multiple_of(i * per_row, 8), per_row)
     source = columns[0, mine, :]
@@ -289,6 +313,7 @@
         add(s, lanes_of(recv.at[0], s) - 1)
         return 0
 
+    load_updated.wait()
     lax.fori_loop(0, early, add_step, 0)
     rest = pl.ds(0, devices - 1)
     pltpu.make_async_copy(send.at[:, rest, :], send.at[:, rest, :], ssem).wait()
@@ -394,8 +419,12 @@
             pltpu.VMEM(edge_tiles.shape, I32),
             pltpu.SMEM(proposals.shape, I32),
             pltpu.VMEM(proposals.shape, I32),
+            pltpu.VMEM(proposals.shape, I32),
             pltpu.VMEM(flags.shape, I32),
-            pltpu.VMEM((2, tiles * LANES), I32),
+            pltpu.VMEM((2, tiles, LANES), I32),
+            pltpu.VMEM((2, 5, tiles, LANES), F32),
+            pltpu.VMEM((2, LANES, tiles * LANES), BF),
+            pltpu.VMEM((2, tiles, LANES), F32),
             pltpu.VMEM(edge_tiles.shape, I32),
             small,
             small,
@@ -413,7 +442,7 @@
             pltpu.VMEM((8, LANES), F32),
             pltpu.VMEM((col_n, 8, LANES), F32),
             dma((4,)),
-            dma((6,)),
+            dma((7,)),
             dma,
             dma((row_n,)),
             dma,
@@ -430,12 +459,29 @@
     ])
 
 
+def finish_kernel(updated_in, cost_in, accepted_in, updated, cost, accepted, sem):
+    copy = pltpu.make_async_copy(updated_in, updated, sem)
+    copy.start()
+    cost[...] = cost_in[...]
+    accepted[...] = accepted_in[...]
+    copy.wait()
+
+
 def per_device(counts, labels, edge_tiles, proposals, accept_flags):
     row_n = lax.axis_size("row")
     col_n = lax.axis_size("col")
-    updated, cost, accepted = ingest(
-        proposals, edge_tiles, accept_flags.reshape(1, -1), labels, counts, row_n, col_n
-    )
+    flags = accept_flags.reshape(1, -1)
+    parts = ingest(proposals, edge_tiles, flags, labels, counts, row_n, col_n)
+    vm = pl.BlockSpec(memory_space=pltpu.VMEM)
+    out16 = jax.ShapeDtypeStruct(flags.shape, F32)
+    updated, cost, accepted = pl.pallas_call(
+        finish_kernel,
+        out_shape=(jax.ShapeDtypeStruct(counts.shape, F32), out16, out16),
+        in_specs=[vm] * 3,
+        out_specs=(pl.BlockSpec(memory_space=pltpu.HBM), vm, vm),
+        scratch_shapes=[pltpu.SemaphoreType.DMA],
+        compiler_params=pltpu.CompilerParams(vmem_limit_bytes=8 << 20),
+    )(*parts)
     return updated, cost.reshape(-1), accepted.reshape(-1)
 
 

time: 46.4 us -> 43 us (0.927)
  local copies, waits for them, and re-layouts: 2.34 us -> 0 us
  Pallas kernels: 43.3 us -> 42.2 us
    pallas_call x1, Pallas kernels: 43.3 us -> 40.4 us  [ingest(): pl.pallas_call(functools.partial(ingest_kernel, row_n, col_n, 6), out_sha...]
    unnamed x3 -> x0, local copies, waits for them, and re-layouts: 2.34 us -> none
    pallas_call x0 -> x1, Pallas kernels: none -> 1.84 us  [per_device(): pl.pallas_call(finish_kernel, out_shape=(jax.ShapeDtypeStruct(counts.shap...]
where the time goes in v4:
time: 43 us; the launch traced here: 42.9 us
  Pallas kernels  42.2 us (98%)
  between operations  0.64 us (1%)
    pallas_call x1, Pallas kernels, ingest(): pl.pallas_call(functools.partial(ingest_kernel, row_n, col_n, 6), out_sha...  40.4 us
    pallas_call x1, Pallas kernels, per_device(): pl.pallas_call(finish_kernel, out_shape=(jax.ShapeDtypeStruct(counts.shap...  1.84 us

profile of v4, /device:TPU:1, one launch (start us, length us, event | category | flops | bytes accessed | tf_op | source)
XLA Modules:
  0.0 42.9 jit_solution(11149411485571835946)
XLA Ops:
  0.6 40.4 %shard_map.76 = (f32[1024,512]{1,0:T(8,128)S(1)}, f32[1,16]{1,0:T(1,128)S(1)}, f32[1,16]{1,0:T(1,128)S(1)}) custom-call(s32[2,256]{1,0:T(2,128)} %proposals_in.1, s32[32,2,128]{2,1,0:T(2,128)} %edges_in.1, s32[1,16]{1,0:T(1,128)} %bitcast.5, s32[7680,128]{1,0:T(8,128)} %bitcast.4, f32[1024,512]{1,0:T(8,128)} %counts_in.1), custom_call_target="tpu_custom_call" | custom-call | tf_op jit(solution)/shard_map/pallas_call | solution.py:411
  41.0 1.8 %shard_map.77 = (f32[1024,512]{1,0:T(8,128)}, f32[1,16]{1,0:T(1,128)}, f32[1,16]{1,0:T(1,128)}) custom-call(f32[1024,512]{1,0:T(8,128)S(1)} %get-tuple-element.9.updated_in, f32[1,16]{1,0:T(1,128)S(1)} %get-tuple-element.10.cost_in, f32[1,16]{1,0:T(1,128)S(1)} %get-tuple-element.11.accepted_in), custom_call_target="tpu_custom_call" | custom-call | tf_op jit(solution)/shard_map/pallas_call | solution.py:477

commit v5 on v4

--- a/solution.py
+++ b/solution.py
@@ -161,19 +161,23 @@
 
 
 STEP = 16
+TABLE_PARTS = 6
 
 
 def ingest_kernel(
     row_n, col_n, early, proposals_in, edges_in, flags_in, table_in, counts_in,
     updated, cost_out, accepted_out,
     table, counts, evm, psm, pvm, near, flags, lab, enc, hot, slots, hi, s0, s1, s2, s3, g, send, recv, tails, acc,
-    columns, picked, col_hot, arrived, packed, finals,
-    hsem, lsem, ssem, rsem, essem, ersem, fssem, frsem,
+    columns, picked, col_hot, halves, merged, arrived, packed, finals,
+    hsem, lsem, tsem, ssem, rsem, essem, ersem, fssem, frsem,
 ):
     devices = row_n * col_n
     i = lax.axis_index("row")
     j = lax.axis_index("col")
     me = i * col_n + j
+    place_of = lax.rem(j, 4) * (col_n // 4) + j // 4
+    my_slot = place_of * row_n + i
+    my_group = my_slot // STEP
     rows_tile, cols_tile = counts.shape
     props = pvm.shape[1]
     per_row = props // row_n
@@ -181,7 +185,8 @@
     sms = (s0, s1, s2, s3)
     barrier = pltpu.get_barrier_semaphore()
 
-    load_table = pltpu.make_async_copy(table_in, table, lsem.at[0])
+    pieces = [pl.ds(k * (table.shape[0] // TABLE_PARTS), table.shape[0] // TABLE_PARTS) for k in range(TABLE_PARTS)]
+    load_table = [pltpu.make_async_copy(table_in.at[p], table.at[p], tsem.at[k]) for k, p in enumerate(pieces)]
     load_counts = pltpu.make_async_copy(counts_in, counts, lsem.at[1])
     load_edges = pltpu.make_async_copy(edges_in, evm, lsem.at[2])
     others = (
@@ -191,7 +196,8 @@
     load_edges.start()
     load_updated = pltpu.make_async_copy(counts_in, updated, lsem.at[6])
     load_near = pltpu.make_async_copy(near, psm, lsem.at[4])
-    load_table.start()
+    for load in load_table:
+        load.start()
     for load in others:
         load.start()
 
@@ -216,7 +222,8 @@
             line = pvm[side : side + 1, h * LANES : (h + 1) * LANES]
             columns[side, h * LANES : (h + 1) * LANES, :] = jnp.broadcast_to(line, (LANES, LANES)).T
     load_near.wait()
-    load_table.wait()
+    for load in load_table:
+        load.wait()
     load_counts.start()
     load_updated.start()
     gather_labels(evm, table, lab, hi, sms, g, hsem)
@@ -229,9 +236,9 @@
             at = pl.ds(d[0] * col_n + d[1], 1)
             pltpu.make_async_remote_copy(
                 src_ref=send.at[:, at, :],
-                dst_ref=recv.at[:, pl.ds(me, 1), :],
+                dst_ref=recv.at[:, pl.ds(my_slot, 1), :],
                 send_sem=ssem,
-                recv_sem=rsem.at[i],
+                recv_sem=rsem.at[my_group],
                 device_id=d,
                 device_id_type=MESH,
             ).start()
@@ -239,7 +246,7 @@
 
     push(0, 0, 1)
     lax.fori_loop(1, row_n, push, 0)
-    recv[:, pl.ds(me, 1), :] = send[:, pl.ds(me, 1), :]
+    recv[:, pl.ds(my_slot, 1), :] = send[:, pl.ds(me, 1), :]
     load_counts.wait()
 
     def pick(u, _):
@@ -276,33 +283,58 @@
         ).astype(F8)
         picked[...] += lax.dot_general(match, hot, NT, preferred_element_type=F32)
 
-    part = recv.at[:, pl.ds(0, col_n - 1), :]
-    pltpu.make_async_copy(part, part, rsem.at[i]).wait()
-    small(i, lanes_of(recv.at[0], i) - 1, lanes_of(recv.at[1], i))
-
-    def arrive(k, _):
-        s = lax.rem(i - k + row_n, row_n)
-        part = recv.at[:, pl.ds(0, col_n), :]
-        pltpu.make_async_copy(part, part, rsem.at[s]).wait()
+    groups = devices // STEP
+
+    def arrive(s, _):
+        @pl.when(s == my_group)
+        def _():
+            part = recv.at[:, pl.ds(0, STEP - 1), :]
+            pltpu.make_async_copy(part, part, rsem.at[s]).wait()
+
+        @pl.when(s != my_group)
+        def _():
+            part = recv.at[:, pl.ds(0, STEP), :]
+            pltpu.make_async_copy(part, part, rsem.at[s]).wait()
+
         small(s, lanes_of(recv.at[0], s) - 1, lanes_of(recv.at[1], s))
         return 0
 
-    lax.fori_loop(1, row_n, arrive, 0)
+    lax.fori_loop(0, groups, arrive, 0)
     tails[...] = recv[2].T
     last_rows = jnp.concatenate([tails[q : q + 1] for q in range(16)], 1) - 1
     last_cols = jnp.concatenate([tails[q : q + 1] for q in range(16, 32)], 1)
-    small(row_n, last_rows, last_cols)
-
-    for k in range(1, row_n):
-        d = lax.rem(i + k, row_n)
-        pltpu.make_async_remote_copy(
-            src_ref=picked.at[pl.ds(pl.multiple_of(d * per_row, 8), per_row), :],
-            dst_ref=arrived.at[i],
-            send_sem=essem,
-            recv_sem=ersem,
-            device_id=(d, j),
+    small(groups, last_rows, last_cols)
+
+    x = i // 2
+    core = lax.rem(i, 2)
+    chips = row_n // 2
+
+    def chunk(k, c):
+        return pl.ds(pl.multiple_of((lax.rem(x + k, chips) * 2 + c) * per_row, 8), per_row)
+
+    def first(k):
+        return pltpu.make_async_remote_copy(
+            src_ref=picked.at[chunk(k, 1 - core), :],
+            dst_ref=halves.at[k],
+            send_sem=essem.at[k],
+            recv_sem=ersem.at[k],
+            device_id=(x * 2 + 1 - core, j),
             device_id_type=MESH,
-        ).start()
+        )
+
+    def second(k):
+        return pltpu.make_async_remote_copy(
+            src_ref=merged.at[k],
+            dst_ref=arrived.at[k],
+            send_sem=essem.at[chips + k],
+            recv_sem=ersem.at[chips + k],
+            device_id=(lax.rem(x + k, chips) * 2 + core, j),
+            device_id_type=MESH,
+        )
+
+    far_first = (2, 1, 3, 0)
+    for k in far_first:
+        first(k).start()
 
     def add(s, rows):
         updated[...] += lax.dot_general(
@@ -314,15 +346,22 @@
         return 0
 
     load_updated.wait()
-    lax.fori_loop(0, early, add_step, 0)
+    lax.fori_loop(0, 1, add_step, 0)
+    for k in far_first:
+        first(k).wait_recv()
+        merged[k] = picked[chunk(k, core), :] + halves[k]
+        if k > 0:
+            second(k).start()
+    lax.fori_loop(1, early, add_step, 0)
     rest = pl.ds(0, devices - 1)
     pltpu.make_async_copy(send.at[:, rest, :], send.at[:, rest, :], ssem).wait()
 
-    most = pl.ds(0, row_n - 1)
-    pltpu.make_async_copy(arrived.at[most], arrived.at[most], ersem).wait()
-    pltpu.make_async_copy(arrived.at[most], arrived.at[most], essem).wait()
-    arrived[i] = picked[mine, :]
-    other = jnp.sum(arrived[...], axis=0)
+    other = merged[0]
+    for k in range(chips):
+        first(k).wait_send()
+        if k > 0:
+            second(k).wait()
+            other += arrived[k]
     own = picked[props:, :]
     where_at = lax.broadcasted_iota(I32, own.shape, 1) + j * cols_tile
     wide4 = cols_tile // LANES
@@ -359,8 +398,8 @@
     def _():
         finals[j] = packed[...]
 
-    lax.fori_loop(early, row_n, add_step, 0)
-    add(row_n, jnp.concatenate([tails[q : q + 1] for q in range(16)], 1) - 1)
+    lax.fori_loop(early, groups, add_step, 0)
+    add(groups, jnp.concatenate([tails[q : q + 1] for q in range(16)], 1) - 1)
 
     @pl.when(home == i)
     def _():
@@ -409,7 +448,7 @@
     dma = pltpu.SemaphoreType.DMA
     out16 = pltpu.VMEM(flags.shape, F32)
     return pl.pallas_call(
-        functools.partial(ingest_kernel, row_n, col_n, 6),
+        functools.partial(ingest_kernel, row_n, col_n, 5),
         out_shape=(pltpu.VMEM(counts.shape, F32), out16, out16),
         in_specs=[anywhere] * 5,
         out_specs=(vm, vm, vm),
@@ -437,16 +476,19 @@
             pltpu.VMEM((576, LANES), F32),
             pltpu.VMEM((2, props, LANES), I32),
             pltpu.VMEM((props + per_row, cols_tile), F32),
-            pltpu.VMEM((row_n + 1, cols_tile, STEP * LANES), F8),
-            pltpu.VMEM((row_n, per_row, cols_tile), F32),
+            pltpu.VMEM((devices // STEP + 1, cols_tile, STEP * LANES), F8),
+            pltpu.VMEM((row_n // 2, per_row, cols_tile), F32),
+            pltpu.VMEM((row_n // 2, per_row, cols_tile), F32),
+            pltpu.VMEM((row_n // 2, per_row, cols_tile), F32),
             pltpu.VMEM((8, LANES), F32),
             pltpu.VMEM((col_n, 8, LANES), F32),
             dma((4,)),
             dma((7,)),
+            dma((TABLE_PARTS,)),
             dma,
+            dma((devices // STEP,)),
             dma((row_n,)),
-            dma,
-            dma,
+            dma((row_n,)),
             dma,
             dma,
         ],

time: 43 us -> 42 us (0.977)
  Pallas kernels: 42.2 us -> 41.2 us
    pallas_call x1, Pallas kernels: 40.4 us -> 39.4 us  [ingest(): pl.pallas_call(functools.partial(ingest_kernel, row_n, col_n, 5), out_sha...]
where the time goes in v5:
time: 42 us; the launch traced here: 41.9 us
  Pallas kernels  41.2 us (98%)
  between operations  0.64 us (2%)
    pallas_call x1, Pallas kernels, ingest(): pl.pallas_call(functools.partial(ingest_kernel, row_n, col_n, 5), out_sha...  39.4 us
    pallas_call x1, Pallas kernels, per_device(): pl.pallas_call(finish_kernel, out_shape=(jax.ShapeDtypeStruct(counts.shap...  1.84 us

profile of v5, /device:TPU:1, one launch (start us, length us, event | category | flops | bytes accessed | tf_op | source)
XLA Modules:
  0.0 41.9 jit_solution(9722286344147005678)
XLA Ops:
  0.6 39.4 %shard_map.76 = (f32[1024,512]{1,0:T(8,128)S(1)}, f32[1,16]{1,0:T(1,128)S(1)}, f32[1,16]{1,0:T(1,128)S(1)}) custom-call(s32[2,256]{1,0:T(2,128)} %proposals_in.1, s32[32,2,128]{2,1,0:T(2,128)} %edges_in.1, s32[1,16]{1,0:T(1,128)} %bitcast.5, s32[7680,128]{1,0:T(8,128)} %bitcast.4, f32[1024,512]{1,0:T(8,128)} %counts_in.1), custom_call_target="tpu_custom_call" | custom-call | tf_op jit(solution)/shard_map/pallas_call | solution.py:450
  40.0 1.8 %shard_map.77 = (f32[1024,512]{1,0:T(8,128)}, f32[1,16]{1,0:T(1,128)}, f32[1,16]{1,0:T(1,128)}) custom-call(f32[1024,512]{1,0:T(8,128)S(1)} %get-tuple-element.9.updated_in, f32[1,16]{1,0:T(1,128)S(1)} %get-tuple-element.10.cost_in, f32[1,16]{1,0:T(1,128)S(1)} %get-tuple-element.11.accepted_in), custom_call_target="tpu_custom_call" | custom-call | tf_op jit(solution)/shard_map/pallas_call | solution.py:519
